TPU v7x, 128 devices: a whole 4x4x4 slice. The times are simulated.
128 devices in a mesh: frame: 8 (over y, core), module: 16 (over z, x).
Axes of the slice: x: 4, y: 4, z: 4, core: 2. Of those that a mesh axis runs over, the one named last changes fastest.
Arguments:
- frames: bfloat16 [2048, 196608], P('frame', 'module'), may hold values from -6 to 6
- weights: bfloat16 [1536, 512, 128], P('module'), may hold values from 0 to 0.25
- monitor: float32 [2048], P('frame'), may hold values from 0.5 to 2
- coverage: int32 [16, 96], replicated, may hold values from 0 to 255, as said below
- block_slot: int32 [16, 96], P('module'), may hold values from 0 to 95, each once within a row
- angle_index: int32 [4], replicated, may hold values from 0 to 179
Outputs:
- slices: bfloat16 [2, 8, 16, 128, 8192], P(None, 'frame', 'module')
Inputs may be any that keep to these rules, and one draw needn't show every extreme that they name: `coverage`: row m holds 96 consecutive tile numbers s, s + 1, ... taken modulo 256, in order, for a start s of its own. `block_slot`: each row is a permutation.
All inputs are finite; a program needn't handle non-finite values.
Results may differ from a plain program's by a relative error of at most 0.0055.
Values sent between devices are 32-bit elements; how exact they have to be, the bound alone decides.
No kernel may reach another device: no remote copies, remote signals or barrier semaphores. Data moves between devices by JAX's collectives and lax.ppermute only.
A program may use at most 192 MiB of HBM per device.

v0:
```python
import math

import jax
import jax.numpy as jnp
from jax import lax
from jax.sharding import PartitionSpec as P

TRANS = 512
ASTEPS = 180
ROWS = 16
NTILE = 256


def ramp_table(length):
    places = jnp.arange(length, dtype=jnp.int32)
    offset = places[:, None] - places[None, :]
    is_odd = offset % 2 != 0
    scaled = math.pi * offset.astype(jnp.float32)
    safe_den = jnp.where(is_odd, scaled, jnp.float32(1.0))
    return jnp.where(
        offset == 0,
        jnp.float32(0.25),
        jnp.where(is_odd, -1.0 / (safe_den * safe_den), jnp.float32(0.0)),
    )


def spot_table(angle_index, row_count, length):
    theta_rad = angle_index.astype(jnp.float32) * (math.pi / ASTEPS)
    centre = (length - 1) / 2.0
    across = jnp.arange(length, dtype=jnp.float32) - centre
    down_pos = jnp.arange(row_count, dtype=jnp.float32) - (row_count - 1) / 2.0
    spot_grid = (
        across[None, None, :] * jnp.cos(theta_rad)[:, None, None]
        + down_pos[None, :, None] * jnp.sin(theta_rad)[:, None, None]
        + centre
    )
    return spot_grid.reshape(angle_index.shape[0], row_count * length)


def on_device(frames, weights, monitor, coverage, block_slot, angle_index):
    groups = lax.axis_size("frame")
    modules = lax.axis_size("module")
    module_pos = lax.axis_index("module")
    fr_dev, pixel_count = frames.shape
    slot_count, group_pixels, tile_width = weights.shape
    group_count = pixel_count // group_pixels
    splits = slot_count // group_count
    local_tiles = NTILE // modules
    grouped = frames.reshape(fr_dev, group_count, group_pixels)
    tile_weights = weights.reshape(group_count, splits, group_pixels, tile_width)
    block_bins = jnp.einsum(
        "fgp,gspc->gsfc", grouped, tile_weights, preferred_element_type=jnp.float32
    )
    block_bins = block_bins.reshape(slot_count, fr_dev, tile_width) / monitor[None, :, None]
    slot_rank = jnp.arange(slot_count, dtype=jnp.int32)
    own_slots = block_slot[0]
    slot_block = jnp.sum(
        jnp.where(own_slots[None, :] == slot_rank[:, None], slot_rank[None, :], 0), axis=1
    )
    first_tile = coverage[module_pos, 0]
    rows_here = jnp.arange(local_tiles * lax.axis_size("module"), dtype=jnp.int32)
    tile_ids = rows_here % local_tiles * modules + rows_here // local_tiles
    slot_ids = (tile_ids - first_tile) % NTILE
    inside = slot_ids < slot_count
    picked = jnp.take(block_bins, slot_block[jnp.minimum(slot_ids, slot_count - 1)], axis=0)
    owned_bins = lax.psum_scatter(
        jnp.where(inside[:, None, None], picked, 0.0), "module", scatter_dimension=0, tiled=True
    )
    tile_rounds = local_tiles // groups
    stacked = owned_bins.reshape(tile_rounds, groups, fr_dev, tile_width)
    angles = angle_index.shape[0]
    column_count = ROWS * TRANS
    ramp_filter = ramp_table(TRANS)
    spot_grid = spot_table(angle_index, ROWS, TRANS)
    positions = jnp.arange(TRANS, dtype=jnp.float32)

    def interp_rows(spot_line):
        return jnp.maximum(0.0, 1.0 - jnp.abs(spot_line[None, :] - positions[:, None])).astype(
            jnp.bfloat16
        )

    tables = lax.map(interp_rows, spot_grid)
    sinogram = lax.all_to_all(stacked, "frame", split_axis=1, concat_axis=2, tiled=True)
    item_count = sinogram.shape[0]
    sino_lines = sinogram.reshape(item_count, angles, TRANS, tile_width)
    filtered = jnp.einsum(
        "iapc,pq->aicq", sino_lines, ramp_filter, precision=lax.Precision.HIGHEST
    ).astype(jnp.bfloat16)
    filtered = filtered.reshape(angles, item_count * tile_width, TRANS)

    def add_angle(angle_pos, summed):
        angle_rows = lax.dynamic_index_in_dim(filtered, angle_pos, 0, keepdims=False)
        angle_table = lax.dynamic_index_in_dim(tables, angle_pos, 0, keepdims=False)
        return summed + jnp.dot(angle_rows, angle_table, preferred_element_type=jnp.float32)

    summed = lax.fori_loop(
        0, angles, add_angle, jnp.zeros((item_count * tile_width, column_count), jnp.float32)
    )
    slices = (summed * (math.pi / angles)).astype(jnp.bfloat16)
    return slices.reshape(item_count, 1, 1, tile_width, column_count)


def solution(mesh):
    placed = (
        P("frame", "module"),
        P("module", None, None),
        P("frame"),
        P(),
        P("module", None),
        P(),
    )
    return jax.shard_map(
        on_device,
        mesh=mesh,
        in_specs=placed,
        out_specs=P(None, "frame", "module", None, None),
        check_vma=False,
    )
```

profile of v0, /device:TPU:1, one launch (start us, length us, event | category | flops | bytes accessed | tf_op | source)
XLA Modules:
  0.0 397.3 jit_solution(14483103444126011524)
XLA Ops:
  8.4 0.8 select_reduce_fusion
  9.2 1.9 gather_fusion
  11.8 8.2 %copy.45 = bf16[32,8,24,512]{3,2,1,0:T(8,128)(2,1)} copy(bf16[32,8,24,512]{3,1,2,0:T(8,128)(2,1)} %bitcast.45) | data formatting | bytes 12582912
  20.0 16.4 %fusion.12 = f32[24,4,128,256]{3,2,1,0:T(8,128)} fusion(bf16[24,4,512,128]{3,2,1,0:T(8,128)(2,1)} %bitcast.44, bf16[256,24,512,1]{2,1,0,3:T(8,128)(2,1)} %bitcast.43), kind=kOutput, calls=%fused_computation.18 | convolution fusion | flops 3221225472 | bytes 31457280 | tf_op jit(solution)/shard_map/fgp,gspc->gsfc/dot_general | solution.py:51
  36.4 12.6 %copy.34 = f32[96,256,128]{2,1,0:T(8,128)} copy(f32[96,256,128]{1,2,0:T(8,128)} %bitcast.42) | data formatting | bytes 25165824 | tf_op jit(solution)/shard_map/reshape | solution.py:54
  49.0 11.4 %broadcast_divide_fusion = f32[96,256,128]{2,1,0:T(8,128)} fusion(f32[96,256,128]{2,1,0:T(8,128)} %copy.34, f32[256]{0:T(256)S(1)} %copy-done.2), kind=kLoop, calls=%fused_computation.20 | loop fusion | flops 3145728 | bytes 25166848 | tf_op jit(solution)/shard_map/div | solution.py:54
  60.4 19.1 %gather_fusion.1 = f32[256,256,128]{2,1,0:T(8,128)} fusion(f32[96,256,128]{2,1,0:T(8,128)} %broadcast_divide_fusion, s32[1024]{0:T(1024)S(1)} %pad_clamp_fusion), kind=kCustom, calls=%fused_computation.1 | custom fusion | bytes 67109888 | tf_op jit(solution)/shard_map/jit(_take)/gather | solution.py:65
  79.5 24.3 %select_select_fusion = f32[256,256,128]{2,1,0:T(8,128)} fusion(f32[256,256,128]{2,1,0:T(8,128)} %gather_fusion.1, pred[256]{0:T(512)(128)(4,1)S(1)} %get-tuple-element.147, pred[256]{0:T(512)(128)(4,1)S(1)} %get-tuple-element.148), kind=kLoop, calls=%fused_computation.16 | loop fusion | flops 16777216 | bytes 67109376 | tf_op jit(solution)/shard_map/jit(_where)/select_n | solution.py:67
  104.8 197.3 %reduce-scatter.2.cloned.1.call-done = f32[16,256,128]{2,1,0:T(8,128)} async-done(((f32[256,256,128]{2,1,0:T(8,128)}), f32[16,256,128]{2,1,0:T(8,128)}) %reduce-scatter.2.cloned.1.call-update) | async-done | bytes 2097168 | tf_op jit(solution)/shard_map/reduce_scatter | solution.py:66
  302.1 3.1 copy.35
  305.2 5.4 %all-to-all-start = ((f32[2,8,256,128]{3,2,0,1:T(8,128)}), f32[2,8,256,128]{3,2,0,1:T(8,128)S(1)}, u32[]{:S(2)}, u32[]{:S(2)}) async-start(f32[2,8,256,128]{3,2,0,1:T(8,128)} %copy.35), calls=%async_computation.1 | async-start | bytes 4194304 | tf_op jit(solution)/shard_map/all_to_all | solution.py:83
  310.7 24.3 %while.25 = (s32[]{:T(128)}, bf16[4,512,8192]{2,1,0:T(8,128)(2,1)}, f32[4,8192]{1,0:T(4,128)S(1)}, s32[]{:T(128)}) while((s32[]{:T(128)}, bf16[4,512,8192]{2,1,0:T(8,128)(2,1)}, f32[4,8192]{1,0:T(4,128)S(1)}, s32[]{:T(128)}) %tuple.59), condition=%wide.region_3.4_spmd.clone, body=%wide.region_2.3_spmd.clone.sunk | while | flops 20971520 | bytes 8487481 | solution.py:82
  310.7 6.1 %fusion.68 = bf16[4,512,8192]{2,1,0:T(8,128)(2,1)} fusion(bf16[4,512,8192]{2,1,0:T(8,128)(2,1)} %get-tuple-element.198, s32[]{:T(128)} %get-tuple-element.197, f32[8192]{0:T(1024)S(1)} %bitcast.47), kind=kLoop, calls=%fused_computation.8.clone.1 | loop fusion | flops 20971520 | bytes 8421888 | tf_op jit(solution)/shard_map/while/body/jit(dynamic_update_index_in_dim)/dynamic_update_slice | solution.py:82
  316.8 6.0 %fusion.68 = bf16[4,512,8192]{2,1,0:T(8,128)(2,1)} fusion(bf16[4,512,8192]{2,1,0:T(8,128)(2,1)} %get-tuple-element.198, s32[]{:T(128)} %get-tuple-element.197, f32[8192]{0:T(1024)S(1)} %bitcast.47), kind=kLoop, calls=%fused_computation.8.clone.1 | loop fusion | flops 20971520 | bytes 8421888 | tf_op jit(solution)/shard_map/while/body/jit(dynamic_update_index_in_dim)/dynamic_update_slice | solution.py:82
  322.8 6.1 %fusion.68 = bf16[4,512,8192]{2,1,0:T(8,128)(2,1)} fusion(bf16[4,512,8192]{2,1,0:T(8,128)(2,1)} %get-tuple-element.198, s32[]{:T(128)} %get-tuple-element.197, f32[8192]{0:T(1024)S(1)} %bitcast.47), kind=kLoop, calls=%fused_computation.8.clone.1 | loop fusion | flops 20971520 | bytes 8421888 | tf_op jit(solution)/shard_map/while/body/jit(dynamic_update_index_in_dim)/dynamic_update_slice | solution.py:82
  328.9 6.0 %fusion.68 = bf16[4,512,8192]{2,1,0:T(8,128)(2,1)} fusion(bf16[4,512,8192]{2,1,0:T(8,128)(2,1)} %get-tuple-element.198, s32[]{:T(128)} %get-tuple-element.197, f32[8192]{0:T(1024)S(1)} %bitcast.47), kind=kLoop, calls=%fused_computation.8.clone.1 | loop fusion | flops 20971520 | bytes 8421888 | tf_op jit(solution)/shard_map/while/body/jit(dynamic_update_index_in_dim)/dynamic_update_slice | solution.py:82
  335.0 1.9 all-to-all-done
  337.0 4.0 %fusion.14 = bf16[4,2,128,512]{3,2,0,1:T(8,128)(2,1)S(1)} fusion(f32[2,4,512,128]{3,2,1,0:T(8,128)S(1)} %bitcast.49), kind=kOutput, calls=%fused_computation.25 | convolution fusion | flops 3227254784 | bytes 3145728 | tf_op jit(solution)/shard_map/iapc,pq->aicq/dot_general | solution.py:86
  341.1 43.2 %while.26 = (s32[]{:T(128)}, f32[256,8192]{1,0:T(8,128)}, bf16[4,256,512]{2,1,0:T(8,128)(2,1)S(1)}, bf16[4,512,8192]{2,1,0:T(8,128)(2,1)}, s32[]{:T(128)}, /*index=5*/s32[]{:T(128)}) while((s32[]{:T(128)}, f32[256,8192]{1,0:T(8,128)}, bf16[4,256,512]{2,1,0:T(8,128)(2,1)S(1)}, bf16[4,512,8192]{2,1,0:T(8,128)(2,1)}, s32[]{:T(128)}, ...), condition=%wide.region_5.6_spmd.clone, body=%wide.region_4.5_spmd.clone.sunk | while | flops 2151677952 | bytes 25429068 | solution.py:96
  341.1 9.0 %convolution_add_fusion.2 = f32[256,8192]{1,0:T(8,128)} fusion(f32[256,8192]{1,0:T(8,128)} %get-tuple-element.212, bf16[4,512,8192]{2,1,0:T(8,128)(2,1)} %get-tuple-element.220, s32[]{:T(128)} %get-tuple-element.211, pred[]{:T(512)S(6)} %compare.23, bf16[4,256,512]{2,1,0:T(8,128)(2,1)S(1)} %get-tuple-element.219), kind=kOutput, calls=%fused_computation.10.clone.1 | convolution fusion | flops 2151677952 | bytes 25428992 | tf_op jit(solution)/shard_map/while/body/eval_jaxpr/dot_general | solution.py:94
  350.2 11.4 %convolution_add_fusion.2 = f32[256,8192]{1,0:T(8,128)} fusion(f32[256,8192]{1,0:T(8,128)} %get-tuple-element.212, bf16[4,512,8192]{2,1,0:T(8,128)(2,1)} %get-tuple-element.220, s32[]{:T(128)} %get-tuple-element.211, pred[]{:T(512)S(6)} %compare.23, bf16[4,256,512]{2,1,0:T(8,128)(2,1)S(1)} %get-tuple-element.219), kind=kOutput, calls=%fused_computation.10.clone.1 | convolution fusion | flops 2151677952 | bytes 25428992 | tf_op jit(solution)/shard_map/while/body/eval_jaxpr/dot_general | solution.py:94
  361.5 11.4 %convolution_add_fusion.2 = f32[256,8192]{1,0:T(8,128)} fusion(f32[256,8192]{1,0:T(8,128)} %get-tuple-element.212, bf16[4,512,8192]{2,1,0:T(8,128)(2,1)} %get-tuple-element.220, s32[]{:T(128)} %get-tuple-element.211, pred[]{:T(512)S(6)} %compare.23, bf16[4,256,512]{2,1,0:T(8,128)(2,1)S(1)} %get-tuple-element.219), kind=kOutput, calls=%fused_computation.10.clone.1 | convolution fusion | flops 2151677952 | bytes 25428992 | tf_op jit(solution)/shard_map/while/body/eval_jaxpr/dot_general | solution.py:94
  372.9 11.4 %convolution_add_fusion.2 = f32[256,8192]{1,0:T(8,128)} fusion(f32[256,8192]{1,0:T(8,128)} %get-tuple-element.212, bf16[4,512,8192]{2,1,0:T(8,128)(2,1)} %get-tuple-element.220, s32[]{:T(128)} %get-tuple-element.211, pred[]{:T(512)S(6)} %compare.23, bf16[4,256,512]{2,1,0:T(8,128)(2,1)S(1)} %get-tuple-element.219), kind=kOutput, calls=%fused_computation.10.clone.1 | convolution fusion | flops 2151677952 | bytes 25428992 | tf_op jit(solution)/shard_map/while/body/eval_jaxpr/dot_general | solution.py:94
  384.3 6.2 %multiply_convert_fusion = bf16[256,8192]{1,0:T(8,128)(2,1)} fusion(f32[256,8192]{1,0:T(8,128)} %get-tuple-element.107), kind=kLoop, calls=%fused_computation.17 | loop fusion | flops 4194304 | bytes 12582912 | tf_op jit(solution)/shard_map/convert_element_type | solution.py:99
  (31 shorter events, 3.9 us)
Async XLA Ops:
  6.5 0.7 copy-start
  6.5 295.6 %reduce-scatter.2.cloned.1.call-start = ((), (), s32[]{:S(2)}) async-start(), calls=%async_computation.2 | async-start | bytes 35651584 | tf_op jit(solution)/shard_map/reduce_scatter | solution.py:66
  36.4 12.6 %copy-start.2 = (f32[256]{0:T(256)S(1)}, f32[256]{0:T(256)}, u32[]{:S(2)}) copy-start(f32[256]{0:T(256)} %param.12) | copy-start | bytes 3076
  103.8 0.7 copy-start.3
  305.2 31.6 %all-to-all-start = ((f32[2,8,256,128]{3,2,0,1:T(8,128)}), f32[2,8,256,128]{3,2,0,1:T(8,128)S(1)}, u32[]{:S(2)}, u32[]{:S(2)}) async-start(f32[2,8,256,128]{3,2,0,1:T(8,128)} %copy.35), calls=%async_computation.1 | async-start | bytes 4194304 | tf_op jit(solution)/shard_map/all_to_all | solution.py:83
  384.3 6.2 %copy-start.1 = (s32[16,96]{1,0:T(8,128)S(1)}, s32[16,96]{1,0:T(8,128)}, u32[]{:S(2)}) copy-start(s32[16,96]{1,0:T(8,128)} %param.13) | copy-start | bytes 18436
Sparse Core Ops, SparseCore 0:
  103.9 198.1 reduce-scatter.1
where the time goes:
time: 398 us; the launch traced here: 397 us
  waiting for transfers between devices  199 us (50%)
  other arithmetic  68.5 us (17%)
  matrix products  63.6 us (16%)
  local copies, waits for them, and re-layouts  47.1 us (12%)
  between operations  13.5 us (3%)
  starting transfers between devices  5.43 us (1%)
    reduce_scatter x1, waiting for transfers between devices, on_device(): lax.psum_scatter(jnp.where(inside[:, None, None], picked, 0.0), 'module',...  197 us
    dot_general x4, matrix products, add_angle(): jnp.dot(angle_rows, angle_table, preferred_element_type=jnp.float32)  43.2 us
    select_n x1, other arithmetic, on_device(): jnp.where(inside[:, None, None], picked, 0.0)  24.3 us
    dynamic_update_slice x4, other arithmetic, on_device(): tables = lax.map(interp_rows, spot_grid)  24.2 us
    gather x1, local copies, waits for them, and re-layouts, on_device(): jnp.take(block_bins, slot_block[jnp.minimum(slot_ids, slot_count - 1)], a...  19.1 us
    dot_general x1, matrix products, on_device(): jnp.einsum('fgp,gspc->gsfc', grouped, tile_weights, preferred_element_typ...  16.4 us
    reshape x1, local copies, waits for them, and re-layouts, on_device(): block_bins.reshape(slot_count, fr_dev, tile_width) / monitor[None, :, None]  12.6 us
    div x1, other arithmetic, on_device(): block_bins.reshape(slot_count, fr_dev, tile_width) / monitor[None, :, None]  11.4 us
  transfers between devices with their start and end apart: 2, of which 2 were waited for; matrix products, arithmetic and copies ran while one was open for 6% of the time, Pallas kernels for 0%

commit v1 on v0

v1 whole, which is shorter than its diff:
```python
import functools
import math

import jax
import jax.numpy as jnp
from jax import lax
from jax.experimental import pallas as pl
from jax.experimental.pallas import tpu as pltpu
from jax.sharding import PartitionSpec as P

TRANS = 512
ASTEPS = 180
ROWS = 16
NTILE = 256
SIDE = 4
CHUNKS = (128, 128)
RELAY = (False, False)
FAR = (1, 3, 2)
WINDOW = 256

VMEM = pltpu.MemorySpace.VMEM
MIB = 1 << 20


def ramp_table(length):
    places = jnp.arange(length, dtype=jnp.int32)
    offset = places[:, None] - places[None, :]
    is_odd = offset % 2 != 0
    scaled = math.pi * offset.astype(jnp.float32)
    safe_den = jnp.where(is_odd, scaled, jnp.float32(1.0))
    return jnp.where(
        offset == 0,
        jnp.float32(0.25),
        jnp.where(is_odd, -1.0 / (safe_den * safe_den), jnp.float32(0.0)),
    )


def spot_table(angle_index, row_count, length):
    theta_rad = angle_index.astype(jnp.float32) * (math.pi / ASTEPS)
    centre = (length - 1) / 2.0
    across = jnp.arange(length, dtype=jnp.float32) - centre
    down_pos = jnp.arange(row_count, dtype=jnp.float32) - (row_count - 1) / 2.0
    return (
        across[None, None, :] * jnp.cos(theta_rad)[:, None, None]
        + down_pos[None, :, None] * jnp.sin(theta_rad)[:, None, None]
        + centre
    )


def bin_kernel(slot_ref, cover_ref, mon_ref, fr_ref, wt_ref, *rest, begin):
    outs, (pixels, tiles, hold, sem, out_sem) = rest[:-5], rest[-5:]
    groups = sem.shape[1]
    depth = pixels.shape[1] // groups
    splits = tiles.shape[0] // groups
    width = tiles.shape[2]
    rows, half = pixels.shape[0], hold.shape[2]
    span = hold.shape[1] // (SIDE * SIDE)

    def fetch(g):
        across = pl.ds(pl.multiple_of(g * depth, depth), depth)
        return (
            pltpu.make_async_copy(
                wt_ref.at[pl.ds(g * splits, splits)],
                tiles.at[pl.ds(g * splits, splits)],
                sem.at[0, g],
            ),
            pltpu.make_async_copy(
                fr_ref.at[pl.ds(begin, rows), across], pixels.at[:, across], sem.at[1, g]
            ),
        )

    for g in range(groups):
        for copy in fetch(g):
            copy.start()
    me = lax.axis_index("module")
    z, x = me // SIDE, me % SIDE
    first = cover_ref[me, 0]
    scale = 1.0 / mon_ref[...]

    def one(g, carry):
        for copy in fetch(g):
            copy.wait()
        across = pl.ds(pl.multiple_of(g * depth, depth), depth)
        here = jnp.concatenate([tiles[g * splits + s] for s in range(splits)], axis=1)
        bins = jnp.dot(pixels[:, across], here, preferred_element_type=jnp.float32)
        bins = bins * scale
        for s in range(splits):
            slot = slot_ref[0, g * splits + s]
            owner = (first + slot) & (SIDE * SIDE - 1)
            turn = slot // (SIDE * SIDE)
            away_z = (owner // SIDE - z) & (SIDE - 1)
            away_x = (owner - x) & (SIDE - 1)
            cut = slice(s * width, (s + 1) * width)
            hold[0, (away_x * SIDE + away_z) * span + turn] = bins[:half, cut]
            hold[1, (away_z * SIDE + away_x) * span + turn] = bins[half:, cut]
        return carry

    lax.fori_loop(0, groups, one, 0)
    each = outs[0].shape[0]
    copies = [
        pltpu.make_async_copy(
            hold.at[n // SIDE, pl.ds(n % SIDE * each, each)], out, out_sem.at[n]
        )
        for n, out in enumerate(outs)
    ]
    for copy in copies:
        copy.start()
    for copy in copies:
        copy.wait()


def bin_chunk(block_slot, coverage, frames, weights, monitor, begin, rows):
    pixels = frames.shape[1]
    slots, group_pixels, width = weights.shape
    groups = pixels // group_pixels
    half = rows // 2
    each = slots // SIDE
    smem = pl.BlockSpec(memory_space=pltpu.MemorySpace.SMEM)
    anywhere = pl.BlockSpec(memory_space=pl.ANY)
    in_hbm = pl.BlockSpec(memory_space=pltpu.MemorySpace.HBM)
    return pl.pallas_call(
        functools.partial(bin_kernel, begin=begin),
        out_shape=[jax.ShapeDtypeStruct((each, half, width), jnp.float32)] * (2 * SIDE),
        in_specs=[smem, smem, pl.BlockSpec(memory_space=VMEM), in_hbm, in_hbm],
        out_specs=[anywhere] * (2 * SIDE),
        scratch_shapes=[
            pltpu.VMEM((rows, pixels), frames.dtype),
            pltpu.VMEM(weights.shape, weights.dtype),
            pltpu.VMEM((2, slots, half, width), jnp.float32),
            pltpu.SemaphoreType.DMA((2, groups)),
            pltpu.SemaphoreType.DMA((2 * SIDE,)),
        ],
        compiler_params=pltpu.CompilerParams(vmem_limit_bytes=(26 if begin else 55) * MIB),
        cost_estimate=pl.CostEstimate(
            flops=2 * rows * pixels * slots // groups * width,
            bytes_accessed=2 * slots * group_pixels * width + 6 * rows * pixels,
            transcendentals=0,
        ),
    )(block_slot, coverage, monitor[begin : begin + rows, None], frames, weights)


def merge_kernel(cover_ref, *rest, axis, relay):
    sources, outs = rest[:SIDE], rest[SIDE:]
    span = sources[0].shape[0] // SIDE
    modules = SIDE * SIDE
    tiles = NTILE // modules
    half = tiles // 2
    me = lax.axis_index("module")
    z, x = me // SIDE, me % SIDE
    if relay:
        keep0, keep1, keep3, plus, minus = outs
        parts = [
            (2, 0, plus.at[0]),
            (2, 1, minus.at[0]),
            (1, 0, keep1),
            (1, 1, plus.at[1]),
            (3, 0, minus.at[1]),
            (3, 1, keep3),
            (0, 0, keep0.at[pl.ds(0, half)]),
            (0, 1, keep0.at[pl.ds(half, half)]),
        ]
    else:
        parts = [(e, p, outs[e].at[pl.ds(p * half, half)]) for e in range(SIDE) for p in range(2)]
    for e, part, out in parts:
        begin = []
        for d in range(SIDE):
            if axis == "x":
                source = z * SIDE + ((x - d) & (SIDE - 1))
                owner = ((z + e) & (SIDE - 1)) * SIDE + x
            else:
                source = ((z - d) & (SIDE - 1)) * SIDE + x
                owner = z * SIDE + ((x + e) & (SIDE - 1))
            first = cover_ref[source, 0]
            skip = (owner - first) & (modules - 1)
            begin.append(((first + skip) // modules) & (tiles - 1))

        def one(k, carry, e=e, part=part, begin=begin, out=out):
            total = None
            for d in range(SIDE):
                j = (k + part * half - begin[d]) & (tiles - 1)
                tile = sources[d][e * span + jnp.minimum(j, span - 1)]
                tile = jnp.where(j < span, tile, 0.0)
                total = tile if total is None else total + tile
            out[k] = total
            return carry

        lax.fori_loop(0, half, one, 0)


def merge(coverage, sources, axis, relay):
    each, rows, width = sources[0].shape
    tiles = NTILE // (SIDE * SIDE)
    half = tiles // 2

    def shape(*lead):
        return jax.ShapeDtypeStruct((*lead, rows, width), jnp.float32)

    if relay:
        outs = [shape(tiles), shape(half), shape(half), shape(2, half), shape(2, half)]
    else:
        outs = [shape(tiles)] * SIDE
    return pl.pallas_call(
        functools.partial(merge_kernel, axis=axis, relay=relay),
        out_shape=outs,
        in_specs=[pl.BlockSpec(memory_space=pltpu.MemorySpace.SMEM)]
        + [pl.BlockSpec(memory_space=VMEM)] * SIDE,
        out_specs=[pl.BlockSpec(memory_space=VMEM)] * len(outs),
        compiler_params=pltpu.CompilerParams(vmem_limit_bytes=14 * MIB),
        cost_estimate=pl.CostEstimate(
            flops=4 * 64 * rows * width,
            bytes_accessed=4 * rows * width * (4 * each + 64),
            transcendentals=0,
        ),
    )(coverage, *sources)


def join_kernel(*refs, relay):
    count = 5 if relay else 4
    outs = refs[2 * count :]
    me = lax.axis_index("frame")
    y, core = me // 2, me % 2
    half = refs[0].shape[0] // 2
    for n, out in enumerate(outs):
        owner = ((y + n // 2) & (SIDE - 1)) * 2 + (core ^ (n % 2))
        for side in range(2):
            parts = refs[count * side : count * (side + 1)]
            if relay:
                keep0, plus, minus, far_plus, far_minus = parts
                out[side] = keep0[owner] + minus[1, owner] + far_plus[owner]
                out[2 + side] = keep0[half + owner] + plus[1, owner] + far_minus[owner]
            else:
                for q in range(2):
                    k = q * half + owner
                    out[2 * q + side] = parts[0][k] + parts[1][k] + (parts[2][k] + parts[3][k])


def join(parts, relay):
    tiles, rows, width = parts[0].shape
    half = tiles // 2
    return pl.pallas_call(
        functools.partial(join_kernel, relay=relay),
        out_shape=[jax.ShapeDtypeStruct((4, rows, width), jnp.float32)] * half,
        in_specs=[pl.BlockSpec(memory_space=VMEM)] * len(parts),
        out_specs=[pl.BlockSpec(memory_space=VMEM)] * half,
        compiler_params=pltpu.CompilerParams(vmem_limit_bytes=14 * MIB),
        cost_estimate=pl.CostEstimate(
            flops=8 * half * rows * width,
            bytes_accessed=4 * rows * width * half * 18,
            transcendentals=0,
        ),
    )(*parts)


def split(value):
    high = value.astype(jnp.bfloat16)
    return high, (value - high.astype(jnp.float32)).astype(jnp.bfloat16)


def filter_kernel(ramp_ref, *rest, begin, count):
    lines, out = rest[:count], rest[-1]
    prev = rest[count] if len(rest) == count + 2 else None
    rows = 2 * lines[0].shape[1]
    width = lines[0].shape[2]
    me = lax.axis_index("frame")
    y, core = me // 2, me % 2
    per_group = ramp_ref.shape[0] // 2
    ramp = jnp.concatenate(
        [ramp_ref[pl.ds((core ^ dc) * per_group + begin, rows), :] for dc in range(2)], axis=0
    )
    ramp_high, ramp_low = split(ramp)
    for dy in range(SIDE):
        a = (y - dy) & (SIDE - 1)
        for q in range(2):
            both = [
                lines[2 * dy + dc][2 * q : 2 * q + 2].reshape(rows, width) for dc in range(2)
            ]
            high, low = split(jnp.concatenate(both, axis=0).T)
            total = jnp.dot(high, ramp_high, preferred_element_type=jnp.float32)
            total = total + jnp.dot(high, ramp_low, preferred_element_type=jnp.float32)
            total = total + jnp.dot(low, ramp_high, preferred_element_type=jnp.float32)
            here = slice(q * width, (q + 1) * width)
            if prev is not None:
                total = total + prev[a, here]
            out[a, here] = total.astype(out.dtype)


def ramp_chunk(ramp, lines, prev, begin, last, angles):
    width = lines[0].shape[2]
    length = ramp.shape[0]
    operands = [ramp, *lines] + ([] if prev is None else [prev])
    return pl.pallas_call(
        functools.partial(filter_kernel, begin=begin, count=len(lines)),
        out_shape=jax.ShapeDtypeStruct(
            (angles, 2 * width, length), jnp.bfloat16 if last else jnp.float32
        ),
        in_specs=[pl.BlockSpec(memory_space=VMEM)] * len(operands),
        out_specs=pl.BlockSpec(memory_space=VMEM),
        compiler_params=pltpu.CompilerParams(vmem_limit_bytes=14 * MIB),
        cost_estimate=pl.CostEstimate(
            flops=6 * angles * 2 * width * length * length // 2,
            bytes_accessed=4 * len(lines) * lines[0].size + 8 * angles * width * length,
            transcendentals=0,
        ),
    )(*operands)


def table_kernel(start_ref, spot_ref, out_ref):
    pair = pl.program_id(0)
    strips, angles, window, cols = out_ref.shape[1:]
    rank = lax.broadcasted_iota(jnp.int32, (window, cols), 0)
    for strip in range(strips):
        for a in range(angles):
            n = strip * angles + a
            place = (rank + start_ref[pair, n] * 128).astype(jnp.float32)
            spot = spot_ref[0, n : n + 1, :]
            out_ref[0, strip, a] = jnp.maximum(0.0, 1.0 - jnp.abs(spot - place)).astype(
                jnp.bfloat16
            )


def make_tables(start, spots, angles):
    pairs, count, cols = spots.shape
    strips = count // angles
    return pl.pallas_call(
        table_kernel,
        name="tables",
        out_shape=jax.ShapeDtypeStruct((pairs, strips, angles, WINDOW, cols), jnp.bfloat16),
        grid_spec=pltpu.PrefetchScalarGridSpec(
            num_scalar_prefetch=1,
            grid=(pairs,),
            in_specs=[pl.BlockSpec((1, count, cols), lambda i, start: (i, 0, 0))],
            out_specs=pl.BlockSpec(
                (1, strips, angles, WINDOW, cols), lambda i, start: (i, 0, 0, 0, 0)
            ),
        ),
        compiler_params=pltpu.CompilerParams(vmem_limit_bytes=10 * MIB),
        cost_estimate=pl.CostEstimate(
            flops=5 * pairs * count * WINDOW * cols,
            bytes_accessed=2 * pairs * count * WINDOW * cols,
            transcendentals=0,
        ),
    )(start, spots)


def back_kernel(start_ref, filt_ref, tables, out_ref, done, out_sem, *, scale):
    pairs, strips, angles, _, cols = tables.shape
    cols = cols // 2
    line = done.shape[1] // (2 * pairs)

    def put(pair):
        across = pl.ds(pl.multiple_of(pair * 2 * line, 2 * line), 2 * line)
        return pltpu.make_async_copy(done.at[:, across], out_ref.at[:, across], out_sem.at[pair])

    def one(pair, carry):
        for strip in range(strips):
            total = None
            for a in range(angles):
                begin = pl.multiple_of(start_ref[pair, strip * angles + a] * 128, 128)
                part = jnp.dot(
                    filt_ref[a, :, pl.ds(begin, WINDOW)],
                    tables[pair, strip, a],
                    preferred_element_type=jnp.float32,
                )
                total = part if total is None else total + part
            total = (total * scale).astype(jnp.bfloat16)
            for r in range(2):
                to = pl.multiple_of(pair * 2 * line + r * line + strip * cols, 128)
                done[:, pl.ds(to, cols)] = total[:, r * cols : (r + 1) * cols]
        put(pair).start()
        return carry

    lax.fori_loop(0, pairs, one, 0)
    for pair in range(pairs):
        put(pair).wait()


def back_project(start, filt, tables):
    angles, bins, length = filt.shape
    pairs, strips, _, window, cols = tables.shape
    columns = pairs * 2 * length
    return pl.pallas_call(
        functools.partial(back_kernel, scale=math.pi / angles),
        name="back",
        out_shape=jax.ShapeDtypeStruct((bins, columns), jnp.bfloat16),
        in_specs=[
            pl.BlockSpec(memory_space=pltpu.MemorySpace.SMEM),
            pl.BlockSpec(memory_space=VMEM),
            pl.BlockSpec(memory_space=VMEM),
        ],
        out_specs=pl.BlockSpec(memory_space=pl.ANY),
        scratch_shapes=[
            pltpu.VMEM((bins, columns), jnp.bfloat16),
            pltpu.SemaphoreType.DMA((pairs,)),
        ],
        compiler_params=pltpu.CompilerParams(vmem_limit_bytes=24 * MIB),
        cost_estimate=pl.CostEstimate(
            flops=2 * bins * pairs * strips * angles * window * cols,
            bytes_accessed=2 * tables.size + 2 * bins * columns,
            transcendentals=0,
        ),
    )(start, filt, tables)


def shift(array, axis, by):
    pairs = []
    for z in range(SIDE):
        for x in range(SIDE):
            to = (z, (x + by) % SIDE) if axis == "x" else ((z + by) % SIDE, x)
            pairs.append((z * SIDE + x, to[0] * SIDE + to[1]))
    return lax.ppermute(array, "module", pairs)


def swap(array, by, cross):
    pairs = []
    for y in range(SIDE):
        for core in range(2):
            pairs.append((y * 2 + core, (y + by) % SIDE * 2 + (core ^ cross)))
    return lax.ppermute(array, "frame", pairs)


def on_device(frames, weights, monitor, coverage, block_slot, angle_index):
    angles = angle_index.shape[0]
    spots = spot_table(angle_index, ROWS, TRANS)
    spots = spots.reshape(angles, ROWS // 2, 2, TRANS // 128, 128)
    spots = spots.transpose(1, 3, 0, 2, 4).reshape(ROWS // 2, TRANS // 128 * angles, 256)
    start = jnp.floor(jnp.min(spots, axis=2) / 128.0).astype(jnp.int32)
    start = jnp.clip(start, 0, (TRANS - WINDOW) // 128)

    def first_leg(sent):
        halves = [[sent[0]], [sent[SIDE]]]
        for d in FAR:
            for side, axis in enumerate("xz"):
                halves[side].append((d, shift(sent[side * SIDE + d], axis, d)))
        return [[own] + [a for _, a in sorted(rest, key=lambda p: p[0])] for own, *rest in halves]

    def second_leg(halves, relay):
        parts = []
        kept = []
        for side, (axis, other) in enumerate((("x", "z"), ("z", "x"))):
            outs = merge(coverage, halves[side], axis, relay)
            if relay:
                keep0, keep1, keep3, plus, minus = outs
                kept.append((keep0, keep1, keep3, shift(plus, other, 1), shift(minus, other, -1)))
            else:
                parts += [outs[0]] + [shift(outs[e], other, e) for e in (1, 2, 3)]
        for side, other in enumerate("zx"):
            if relay:
                keep0, keep1, keep3, plus, minus = kept[side]
                far_plus = shift(keep1 + plus[0], other, 1)
                far_minus = shift(keep3 + minus[0], other, -1)
                parts += [keep0, plus, minus, far_plus, far_minus]
        own, *others = join(parts, relay)
        return [own] + [swap(o, n // 2, n % 2) for n, o in enumerate(others, 1)]

    begins = [sum(CHUNKS[:c]) for c in range(len(CHUNKS))]
    sent = [
        bin_chunk(block_slot, coverage, frames, weights, monitor, begin, rows)
        for begin, rows in zip(begins, CHUNKS)
    ]
    filt = None
    arrived = first_leg(sent[0])
    ramp = ramp_table(TRANS)
    tables = make_tables(start, spots, angles)
    for c, begin in enumerate(begins):
        here = arrived
        last = c + 1 == len(CHUNKS)
        if not last:
            extra = (ramp, tables) if c == 0 else ()
            held = []
            for side in range(2):
                ready = sent[c + 1][side * SIDE : (side + 1) * SIDE]
                ready, here[side], extra = lax.optimization_barrier((ready, here[side], extra))
                held += ready
            if c == 0:
                ramp, tables = extra
            arrived = first_leg(held)
        lines = second_leg(here, RELAY[c])
        filt = ramp_chunk(ramp, lines, filt, begin, last, angles)
    slices = back_project(start, filt, tables)
    return slices.reshape(2, 1, 1, slices.shape[0] // 2, slices.shape[1])


def solution(mesh):
    placed = (
        P("frame", "module"),
        P("module", None, None),
        P("frame"),
        P(),
        P("module", None),
        P(),
    )
    return jax.shard_map(
        on_device,
        mesh=mesh,
        in_specs=placed,
        out_specs=P(None, "frame", "module", None, None),
        check_vma=False,
    )
```

time: 398 us -> 206 us (0.52)
  waiting for transfers between devices: 199 us -> 74.9 us
  other arithmetic: 68.5 us -> 1.18 us
  starting transfers between devices: 5.43 us -> 71.2 us
  matrix products: 63.6 us -> 0 us
  Pallas kernels: 0 us -> 47.3 us
  local copies, waits for them, and re-layouts: 47.1 us -> 10.6 us
  between operations: 13.5 us -> 0.48 us
    reduce_scatter x1 -> x0, waiting for transfers between devices: 197 us -> none  [on_device(): lax.psum_scatter(jnp.where(inside[:, None, None], picked, 0.0), 'module',...]
    ppermute x0 -> x38, waiting for transfers between devices: none -> 74.9 us  [the longest x24 65.4 us: shift(): return lax.ppermute(array, 'module', pairs)]
    ppermute x0 -> x38, starting transfers between devices: none -> 71.2 us  [the longest x14 41.7 us: swap(): return lax.ppermute(array, 'frame', pairs)]
    dot_general x6 -> x0, matrix products: 63.6 us -> none  [the longest x4 43.2 us: add_angle(): jnp.dot(angle_rows, angle_table, preferred_element_type=jnp.float32)]
    pallas_call x0 -> x12, Pallas kernels: none -> 47.3 us  [the longest x2 20.3 us: bin_chunk(): pl.pallas_call(functools.partial(bin_kernel, begin=begin), out_shape=[jax...]
    select_n x3 -> x1, other arithmetic: 25 us -> 0.56 us  [ramp_table(): jnp.where(offset == 0, jnp.float32(0.25), jnp.where(is_odd, -1.0 / (safe_...]
    dynamic_update_slice x4 -> x0, other arithmetic: 24.2 us -> none  [on_device(): tables = lax.map(interp_rows, spot_grid)]
    gather x2 -> x0, local copies, waits for them, and re-layouts: 20.9 us -> none  [the longest x1 19.1 us: on_device(): jnp.take(block_bins, slot_block[jnp.minimum(slot_ids, slot_count - 1)], a...]
  transfers between devices with their start and end apart: 2 -> 38, of which waited for: 2 -> 13; matrix products, arithmetic and copies ran while one was open for 6% -> 1% of each run, Pallas kernels for 0% -> 13%
where the time goes in v1:
time: 206 us
  waiting for transfers between devices  74.9 us (36%)
  starting transfers between devices  71.2 us (35%)
  Pallas kernels  47.3 us (23%)
  local copies, waits for them, and re-layouts  10.6 us (5%)
    ppermute x24, waiting for transfers between devices, shift(): return lax.ppermute(array, 'module', pairs)  65.4 us
    ppermute x14, starting transfers between devices, swap(): return lax.ppermute(array, 'frame', pairs)  41.7 us
    ppermute x24, starting transfers between devices, shift(): return lax.ppermute(array, 'module', pairs)  29.5 us
    pallas_call x2, Pallas kernels, bin_chunk(): pl.pallas_call(functools.partial(bin_kernel, begin=begin), out_shape=[jax...  20.3 us
    ppermute x14, waiting for transfers between devices, swap(): return lax.ppermute(array, 'frame', pairs)  9.45 us
    pallas_call x4, Pallas kernels, merge(): pl.pallas_call(functools.partial(merge_kernel, axis=axis, relay=relay), o...  9.34 us
    unnamed x25, local copies, waits for them, and re-layouts  8.63 us
    pallas_call x1, Pallas kernels, back_project(): pl.pallas_call(functools.partial(back_kernel, scale=math.pi / angles), na...  8.28 us
  transfers between devices with their start and end apart: 38, of which 13 were waited for; matrix products, arithmetic and copies ran while one was open for 1% of the time, Pallas kernels for 13%

profile of v1, /device:TPU:1, one launch (start us, length us, event | category | flops | bytes accessed | tf_op | source)
XLA Modules:
  0.0 205.6 jit_solution(3865231955149396164)
XLA Ops:
  1.5 11.3 %shard_map.65 = (f32[24,64,128]{2,1,0:T(8,128)}, f32[24,64,128]{2,1,0:T(8,128)}, f32[24,64,128]{2,1,0:T(8,128)}, f32[24,64,128]{2,1,0:T(8,128)}, f32[24,64,128]{...) custom-call(s32[1,96]{1,0:T(1,128)} %slot_ref.3, s32[16,96]{1,0:T(8,128)} %cover_ref.11, ...), custom_call_target="tpu_custom_call" | custom-call | flops 1610612736 | bytes 22020096 | tf_op jit(solution)/shard_map/pallas_call | solution.py:121
  12.8 2.5 %collective-permute-start = (f32[24,64,128]{2,1,0:T(8,128)}, f32[24,64,128]{2,1,0:T(8,128)S(1)}, u32[]{:S(2)}, u32[]{:S(2)}) collective-permute-start(f32[24,64,128]{2,1,0:T(8,128)} %get-tuple-element.78), channel_id=1, source_target_pairs={{0,4},{1,5},{2,6},{3,7},{4,8},{5,9},{6,10},{7,11},{8,12},{9,13},{1... | collective-permute-start | bytes 2359304 | tf_op jit(solution)/shard_map/ppermute | solution.py:410
  15.3 3.3 %collective-permute-start.1 = (f32[24,64,128]{2,1,0:T(8,128)}, f32[24,64,128]{2,1,0:T(8,128)}, u32[]{:S(2)}, u32[]{:S(2)}) collective-permute-start(f32[24,64,128]{2,1,0:T(8,128)} %get-tuple-element.79), channel_id=1, source_target_pairs={{0,8},{1,9},{2,10},{3,11},{4,12},{5,13},{6,14},{7,15},{8,0},{9,1},... | collective-permute-start | bytes 2359304 | tf_op jit(solution)/shard_map/ppermute | solution.py:410
  20.6 2.5 %collective-permute-start.4 = (f32[24,64,128]{2,1,0:T(8,128)}, f32[24,64,128]{2,1,0:T(8,128)S(1)}, u32[]{:S(2)}, u32[]{:S(2)}) collective-permute-start(f32[24,64,128]{2,1,0:T(8,128)} %get-tuple-element.87), channel_id=1, source_target_pairs={{0,2},{1,3},{2,0},{3,1},{4,6},{5,7},{6,4},{7,5},{8,10},{9,11},{10,... | collective-permute-start | bytes 2359304 | tf_op jit(solution)/shard_map/ppermute | solution.py:410
  23.7 14.7 %collective-permute-done.3.rest_1_ = f32[24,64,128]{2,1,0:T(8,128)S(1)} collective-permute-done((f32[24,64,128]{2,1,0:T(8,128)}, f32[24,64,128]{2,1,0:T(8,128)S(1)}, u32[]{:S(2)}, u32[]{:S(2)}) %collective-permute-start.3) | collective-permute-done | bytes 786464 | tf_op jit(solution)/shard_map/ppermute | solution.py:410
  40.1 6.7 %tables.1 = bf16[8,4,4,256,256]{4,3,2,1,0:T(8,128)(2,1)S(1)} custom-call(s32[8,16]{1,0:T(8,128)S(1)} %copy.22.start_ref, f32[8,16,256]{2,1,0:T(8,128)S(1)} %add_add_fusion.spot_ref), custom_call_target="tpu_custom_call" | custom-call | flops 41943040 | bytes 16777216 | tf_op jit(solution)/shard_map/tables/pallas_call | solution.py:324
  46.9 5.8 %copy-done = bf16[8,4,4,256,256]{4,3,2,1,0:T(8,128)(2,1)} copy-done((bf16[8,4,4,256,256]{4,3,2,1,0:T(8,128)(2,1)}, bf16[8,4,4,256,256]{4,3,2,1,0:T(8,128)(2,1)S(1)}, u32[]{:S(2)}) %copy-start) | copy-done | bytes 16777240
  52.7 2.8 %copy-done.2 = bf16[256,12288]{1,0:T(8,128)(2,1)S(1)} copy-done((bf16[256,12288]{1,0:T(8,128)(2,1)S(1)}, bf16[256,12288]{1,0:T(8,128)(2,1)}, u32[]{:S(2)}) %copy-start.2) | copy-done | bytes 6291480
  55.5 9.0 %shard_map.64 = (f32[24,64,128]{2,1,0:T(8,128)S(1)}, f32[24,64,128]{2,1,0:T(8,128)S(1)}, f32[24,64,128]{2,1,0:T(8,128)S(1)}, f32[24,64,128]{2,1,0:T(8,128)S(1)},...) custom-call(s32[1,96]{1,0:T(1,128)S(1)} %copy-done.6, ...), custom_call_target="tpu_custom_call" | custom-call | flops 1610612736 | bytes 22020096 | tf_op jit(solution)/shard_map/pallas_call | solution.py:121
  66.0 2.9 %shard_map.70 = (f32[16,64,128]{2,1,0:T(8,128)S(1)}, f32[16,64,128]{2,1,0:T(8,128)S(1)}, f32[16,64,128]{2,1,0:T(8,128)S(1)}, f32[16,64,128]{2,1,0:T(8,128)S(1)}) custom-call(s32[16,96]{1,0:T(8,128)S(1)} %copy-done.5, f32[24,64,128]{2,1,0:T(8,128)S(1)} %copy-done.4, f32[24,64,128]{2,1,0:T(8,128)S(1)} %collective-permute-done.rest_1_, ...), custom_call_target="tpu_custom_call" | custom-call | flops 2097152 | bytes 5242880 | tf_op jit(solution)/shard_map/pallas_call | solution.py:202
  73.2 6.9 %collective-permute-done.28.refs_5_ = f32[16,64,128]{2,1,0:T(8,128)S(1)} collective-permute-done((f32[16,64,128]{2,1,0:T(8,128)S(1)}, f32[16,64,128]{2,1,0:T(8,128)S(1)}, u32[]{:S(2)}, u32[]{:S(2)}) %collective-permute-start.28) | collective-permute-done | bytes 524320 | tf_op jit(solution)/shard_map/ppermute | solution.py:410
  80.1 9.2 %collective-permute-done.29.refs_6_ = f32[16,64,128]{2,1,0:T(8,128)S(1)} collective-permute-done((f32[16,64,128]{2,1,0:T(8,128)S(1)}, f32[16,64,128]{2,1,0:T(8,128)S(1)}, u32[]{:S(2)}, u32[]{:S(2)}) %collective-permute-start.29) | collective-permute-done | bytes 524320 | tf_op jit(solution)/shard_map/ppermute | solution.py:410
  93.1 4.2 %collective-permute-done.13.rest_2_ = f32[24,64,128]{2,1,0:T(8,128)S(1)} collective-permute-done((f32[24,64,128]{2,1,0:T(8,128)S(1)}, f32[24,64,128]{2,1,0:T(8,128)S(1)}, u32[]{:S(2)}, u32[]{:S(2)}) %collective-permute-start.13) | collective-permute-done | bytes 786464 | tf_op jit(solution)/shard_map/ppermute | solution.py:410
  97.9 9.1 %collective-permute-done.14.rest_3_ = f32[24,64,128]{2,1,0:T(8,128)S(1)} collective-permute-done((f32[24,64,128]{2,1,0:T(8,128)S(1)}, f32[24,64,128]{2,1,0:T(8,128)S(1)}, u32[]{:S(2)}, u32[]{:S(2)}) %collective-permute-start.14) | collective-permute-done | bytes 786464 | tf_op jit(solution)/shard_map/ppermute | solution.py:410
  108.7 3.0 %collective-permute-start.26 = (f32[16,64,128]{2,1,0:T(8,128)S(1)}, f32[16,64,128]{2,1,0:T(8,128)S(1)}, u32[]{:S(2)}, u32[]{:S(2)}) collective-permute-start(f32[16,64,128]{2,1,0:T(8,128)S(1)} %get-tuple-element.122), channel_id=1, source_target_pairs={{0,8},{1,9},{2,10},{3,11},{4,12},{5,13},{6,14},{7,15},{8,0},{9,1},... | collective-permute-start | bytes 1572872 | tf_op jit(solution)/shard_map/ppermute | solution.py:410
  111.7 11.3 %collective-permute-done.7.rest_2_ = f32[24,64,128]{2,1,0:T(8,128)S(1)} collective-permute-done((f32[24,64,128]{2,1,0:T(8,128)S(1)}, f32[24,64,128]{2,1,0:T(8,128)S(1)}, u32[]{:S(2)}, u32[]{:S(2)}) %collective-permute-start.7) | collective-permute-done | bytes 786464 | tf_op jit(solution)/shard_map/ppermute | solution.py:410
  133.4 8.8 %collective-permute-done.15.refs_5_ = f32[16,64,128]{2,1,0:T(8,128)S(1)} collective-permute-done((f32[16,64,128]{2,1,0:T(8,128)S(1)}, f32[16,64,128]{2,1,0:T(8,128)S(1)}, u32[]{:S(2)}, u32[]{:S(2)}) %collective-permute-start.15) | collective-permute-done | bytes 524320 | tf_op jit(solution)/shard_map/ppermute | solution.py:410
  143.6 15.5 %collective-permute-start.31 = (f32[4,64,128]{2,1,0:T(8,128)S(1)}, f32[4,64,128]{2,1,0:T(8,128)S(1)}, u32[]{:S(2)}, u32[]{:S(2)}) collective-permute-start(f32[4,64,128]{2,1,0:T(8,128)S(1)} %get-tuple-element.133), channel_id=1, source_target_pairs={{0,16},{16,0},{32,48},{48,32},{64,80},{80,64},{96,112},{112,96},{1... | collective-permute-start | bytes 393224 | tf_op jit(solution)/shard_map/ppermute | solution.py:418
  163.2 11.1 %collective-permute-start.35 = (f32[4,64,128]{2,1,0:T(8,128)S(1)}, f32[4,64,128]{2,1,0:T(8,128)S(1)}, u32[]{:S(2)}, u32[]{:S(2)}) collective-permute-start(f32[4,64,128]{2,1,0:T(8,128)S(1)} %get-tuple-element.137), channel_id=1, source_target_pairs={{0,80},{16,64},{32,112},{48,96},{64,16},{80,0},{96,48},{112,32},{1... | collective-permute-start | bytes 393224 | tf_op jit(solution)/shard_map/ppermute | solution.py:418
  183.2 2.4 %collective-permute-start.22 = (f32[4,64,128]{2,1,0:T(8,128)S(1)}, f32[4,64,128]{2,1,0:T(8,128)S(1)}, u32[]{:S(2)}, u32[]{:S(2)}) collective-permute-start(f32[4,64,128]{2,1,0:T(8,128)S(1)} %get-tuple-element.113), channel_id=1, source_target_pairs={{0,80},{16,64},{32,112},{48,96},{64,16},{80,0},{96,48},{112,32},{1... | collective-permute-start | bytes 393224 | tf_op jit(solution)/shard_map/ppermute | solution.py:418
  188.4 2.4 %collective-permute-done.22.rest_5_ = f32[4,64,128]{2,1,0:T(8,128)S(1)} collective-permute-done((f32[4,64,128]{2,1,0:T(8,128)S(1)}, f32[4,64,128]{2,1,0:T(8,128)S(1)}, u32[]{:S(2)}, u32[]{:S(2)}) %collective-permute-start.22) | collective-permute-done | bytes 131104 | tf_op jit(solution)/shard_map/ppermute | solution.py:418
  190.8 2.5 %collective-permute-done.23.rest_6_ = f32[4,64,128]{2,1,0:T(8,128)S(1)} collective-permute-done((f32[4,64,128]{2,1,0:T(8,128)S(1)}, f32[4,64,128]{2,1,0:T(8,128)S(1)}, u32[]{:S(2)}, u32[]{:S(2)}) %collective-permute-start.23) | collective-permute-done | bytes 131104 | tf_op jit(solution)/shard_map/ppermute | solution.py:418
  193.3 2.8 %collective-permute-done.24.rest_7_ = f32[4,64,128]{2,1,0:T(8,128)S(1)} collective-permute-done((f32[4,64,128]{2,1,0:T(8,128)S(1)}, f32[4,64,128]{2,1,0:T(8,128)S(1)}, u32[]{:S(2)}, u32[]{:S(2)}) %collective-permute-start.24) | collective-permute-done | bytes 131104 | tf_op jit(solution)/shard_map/ppermute | solution.py:418
  197.2 8.3 %back.1 = bf16[256,8192]{1,0:T(8,128)(2,1)} custom-call(s32[8,16]{1,0:T(8,128)S(1)} %copy.22.start_ref, bf16[4,256,512]{2,1,0:T(8,128)(2,1)S(1)} %shard_map.73.filt_ref, bf16[8,4,4,256,256]{4,3,2,1,0:T(8,128)(2,1)S(1)} %bitcast.14), custom_call_target="tpu_custom_call" | custom-call | flops 4294967296 | bytes 20971520 | tf_op jit(solution)/shard_map/back/pallas_call | solution.py:381
  (107 shorter events, 46.2 us)
Async XLA Ops:
  12.8 52.3 %collective-permute-start = (f32[24,64,128]{2,1,0:T(8,128)}, f32[24,64,128]{2,1,0:T(8,128)S(1)}, u32[]{:S(2)}, u32[]{:S(2)}) collective-permute-start(f32[24,64,128]{2,1,0:T(8,128)} %get-tuple-element.78), channel_id=1, source_target_pairs={{0,4},{1,5},{2,6},{3,7},{4,8},{5,9},{6,10},{7,11},{8,12},{9,13},{1... | collective-permute-start | bytes 2359304 | tf_op jit(solution)/shard_map/ppermute | solution.py:410
  15.3 49.8 %collective-permute-start.1 = (f32[24,64,128]{2,1,0:T(8,128)}, f32[24,64,128]{2,1,0:T(8,128)}, u32[]{:S(2)}, u32[]{:S(2)}) collective-permute-start(f32[24,64,128]{2,1,0:T(8,128)} %get-tuple-element.79), channel_id=1, source_target_pairs={{0,8},{1,9},{2,10},{3,11},{4,12},{5,13},{6,14},{7,15},{8,0},{9,1},... | collective-permute-start | bytes 2359304 | tf_op jit(solution)/shard_map/ppermute | solution.py:410
  18.6 46.5 %collective-permute-start.2 = (f32[24,64,128]{2,1,0:T(8,128)}, f32[24,64,128]{2,1,0:T(8,128)}, u32[]{:S(2)}, u32[]{:S(2)}) collective-permute-start(f32[24,64,128]{2,1,0:T(8,128)} %get-tuple-element.80), channel_id=1, source_target_pairs={{0,12},{1,13},{2,14},{3,15},{4,0},{5,1},{6,2},{7,3},{8,4},{9,5},{1... | collective-permute-start | bytes 2359304 | tf_op jit(solution)/shard_map/ppermute | solution.py:410
  19.4 19.1 %collective-permute-start.3 = (f32[24,64,128]{2,1,0:T(8,128)}, f32[24,64,128]{2,1,0:T(8,128)S(1)}, u32[]{:S(2)}, u32[]{:S(2)}) collective-permute-start(f32[24,64,128]{2,1,0:T(8,128)} %get-tuple-element.86), channel_id=1, source_target_pairs={{0,1},{1,2},{2,3},{3,0},{4,5},{5,6},{6,7},{7,4},{8,9},{9,10},{10,1... | collective-permute-start | bytes 2359304 | tf_op jit(solution)/shard_map/ppermute | solution.py:410
  20.6 44.5 %collective-permute-start.4 = (f32[24,64,128]{2,1,0:T(8,128)}, f32[24,64,128]{2,1,0:T(8,128)S(1)}, u32[]{:S(2)}, u32[]{:S(2)}) collective-permute-start(f32[24,64,128]{2,1,0:T(8,128)} %get-tuple-element.87), channel_id=1, source_target_pairs={{0,2},{1,3},{2,0},{3,1},{4,6},{5,7},{6,4},{7,5},{8,10},{9,11},{10,... | collective-permute-start | bytes 2359304 | tf_op jit(solution)/shard_map/ppermute | solution.py:410
  38.5 26.6 %collective-permute-start.5 = (f32[24,64,128]{2,1,0:T(8,128)}, f32[24,64,128]{2,1,0:T(8,128)S(1)}, u32[]{:S(2)}, u32[]{:S(2)}) collective-permute-start(f32[24,64,128]{2,1,0:T(8,128)} %get-tuple-element.88), channel_id=1, source_target_pairs={{0,3},{1,0},{2,1},{3,2},{4,7},{5,4},{6,5},{7,6},{8,11},{9,8},{10,9... | collective-permute-start | bytes 2359304 | tf_op jit(solution)/shard_map/ppermute | solution.py:410
  65.1 25.9 %collective-permute-start.12 = (f32[24,64,128]{2,1,0:T(8,128)S(1)}, f32[24,64,128]{2,1,0:T(8,128)S(1)}, u32[]{:S(2)}, u32[]{:S(2)}) collective-permute-start(f32[24,64,128]{2,1,0:T(8,128)S(1)} %get-tuple-element.101), channel_id=1, source_target_pairs={{0,4},{1,5},{2,6},{3,7},{4,8},{5,9},{6,10},{7,11},{8,12},{9,13},{1... | collective-permute-start | bytes 2359304 | tf_op jit(solution)/shard_map/ppermute | solution.py:410
  69.1 20.1 %collective-permute-start.29 = (f32[16,64,128]{2,1,0:T(8,128)S(1)}, f32[16,64,128]{2,1,0:T(8,128)S(1)}, u32[]{:S(2)}, u32[]{:S(2)}) collective-permute-start(f32[16,64,128]{2,1,0:T(8,128)S(1)} %get-tuple-element.130), channel_id=1, source_target_pairs={{0,2},{1,3},{2,0},{3,1},{4,6},{5,7},{6,4},{7,5},{8,10},{9,11},{10,... | collective-permute-start | bytes 1572872 | tf_op jit(solution)/shard_map/ppermute | solution.py:410
  70.8 26.5 %collective-permute-start.13 = (f32[24,64,128]{2,1,0:T(8,128)S(1)}, f32[24,64,128]{2,1,0:T(8,128)S(1)}, u32[]{:S(2)}, u32[]{:S(2)}) collective-permute-start(f32[24,64,128]{2,1,0:T(8,128)S(1)} %get-tuple-element.102), channel_id=1, source_target_pairs={{0,8},{1,9},{2,10},{3,11},{4,12},{5,13},{6,14},{7,15},{8,0},{9,1},... | collective-permute-start | bytes 2359304 | tf_op jit(solution)/shard_map/ppermute | solution.py:410
  71.5 35.5 %collective-permute-start.14 = (f32[24,64,128]{2,1,0:T(8,128)S(1)}, f32[24,64,128]{2,1,0:T(8,128)S(1)}, u32[]{:S(2)}, u32[]{:S(2)}) collective-permute-start(f32[24,64,128]{2,1,0:T(8,128)S(1)} %get-tuple-element.103), channel_id=1, source_target_pairs={{0,12},{1,13},{2,14},{3,15},{4,0},{5,1},{6,2},{7,3},{8,4},{9,5},{1... | collective-permute-start | bytes 2359304 | tf_op jit(solution)/shard_map/ppermute | solution.py:410
  80.1 28.6 %collective-permute-start.6 = (f32[24,64,128]{2,1,0:T(8,128)S(1)}, f32[24,64,128]{2,1,0:T(8,128)S(1)}, u32[]{:S(2)}, u32[]{:S(2)}) collective-permute-start(f32[24,64,128]{2,1,0:T(8,128)S(1)} %get-tuple-element.93), channel_id=1, source_target_pairs={{0,1},{1,2},{2,3},{3,0},{4,5},{5,6},{6,7},{7,4},{8,9},{9,10},{10,1... | collective-permute-start | bytes 2359304 | tf_op jit(solution)/shard_map/ppermute | solution.py:410
  89.2 33.7 %collective-permute-start.7 = (f32[24,64,128]{2,1,0:T(8,128)S(1)}, f32[24,64,128]{2,1,0:T(8,128)S(1)}, u32[]{:S(2)}, u32[]{:S(2)}) collective-permute-start(f32[24,64,128]{2,1,0:T(8,128)S(1)} %get-tuple-element.94), channel_id=1, source_target_pairs={{0,2},{1,3},{2,0},{3,1},{4,6},{5,7},{6,4},{7,5},{8,10},{9,11},{10,... | collective-permute-start | bytes 2359304 | tf_op jit(solution)/shard_map/ppermute | solution.py:410
  91.0 35.9 %collective-permute-start.8 = (f32[24,64,128]{2,1,0:T(8,128)S(1)}, f32[24,64,128]{2,1,0:T(8,128)S(1)}, u32[]{:S(2)}, u32[]{:S(2)}) collective-permute-start(f32[24,64,128]{2,1,0:T(8,128)S(1)} %get-tuple-element.95), channel_id=1, source_target_pairs={{0,3},{1,0},{2,1},{3,2},{4,7},{5,4},{6,5},{7,6},{8,11},{9,8},{10,9... | collective-permute-start | bytes 2359304 | tf_op jit(solution)/shard_map/ppermute | solution.py:410
  97.3 31.8 %collective-permute-start.30 = (f32[16,64,128]{2,1,0:T(8,128)S(1)}, f32[16,64,128]{2,1,0:T(8,128)S(1)}, u32[]{:S(2)}, u32[]{:S(2)}) collective-permute-start(f32[16,64,128]{2,1,0:T(8,128)S(1)} %get-tuple-element.131), channel_id=1, source_target_pairs={{0,3},{1,0},{2,1},{3,2},{4,7},{5,4},{6,5},{7,6},{8,11},{9,8},{10,9... | collective-permute-start | bytes 1572872 | tf_op jit(solution)/shard_map/ppermute | solution.py:410
  107.1 23.1 %collective-permute-start.25 = (f32[16,64,128]{2,1,0:T(8,128)S(1)}, f32[16,64,128]{2,1,0:T(8,128)S(1)}, u32[]{:S(2)}, u32[]{:S(2)}) collective-permute-start(f32[16,64,128]{2,1,0:T(8,128)S(1)} %get-tuple-element.121), channel_id=1, source_target_pairs={{0,4},{1,5},{2,6},{3,7},{4,8},{5,9},{6,10},{7,11},{8,12},{9,13},{1... | collective-permute-start | bytes 1572872 | tf_op jit(solution)/shard_map/ppermute | solution.py:410
  108.7 23.6 %collective-permute-start.26 = (f32[16,64,128]{2,1,0:T(8,128)S(1)}, f32[16,64,128]{2,1,0:T(8,128)S(1)}, u32[]{:S(2)}, u32[]{:S(2)}) collective-permute-start(f32[16,64,128]{2,1,0:T(8,128)S(1)} %get-tuple-element.122), channel_id=1, source_target_pairs={{0,8},{1,9},{2,10},{3,11},{4,12},{5,13},{6,14},{7,15},{8,0},{9,1},... | collective-permute-start | bytes 1572872 | tf_op jit(solution)/shard_map/ppermute | solution.py:410
  126.9 15.3 %collective-permute-start.15 = (f32[16,64,128]{2,1,0:T(8,128)S(1)}, f32[16,64,128]{2,1,0:T(8,128)S(1)}, u32[]{:S(2)}, u32[]{:S(2)}) collective-permute-start(f32[16,64,128]{2,1,0:T(8,128)S(1)} %get-tuple-element.105), channel_id=1, source_target_pairs={{0,1},{1,2},{2,3},{3,0},{4,5},{5,6},{6,7},{7,4},{8,9},{9,10},{10,1... | collective-permute-start | bytes 1572872 | tf_op jit(solution)/shard_map/ppermute | solution.py:410
  130.2 28.9 %collective-permute-start.17 = (f32[16,64,128]{2,1,0:T(8,128)S(1)}, f32[16,64,128]{2,1,0:T(8,128)S(1)}, u32[]{:S(2)}, u32[]{:S(2)}) collective-permute-start(f32[16,64,128]{2,1,0:T(8,128)S(1)} %get-tuple-element.107), channel_id=1, source_target_pairs={{0,3},{1,0},{2,1},{3,2},{4,7},{5,4},{6,5},{7,6},{8,11},{9,8},{10,9... | collective-permute-start | bytes 1572872 | tf_op jit(solution)/shard_map/ppermute | solution.py:410
  132.2 28.1 %collective-permute-start.9 = (f32[16,64,128]{2,1,0:T(8,128)S(1)}, f32[16,64,128]{2,1,0:T(8,128)S(1)}, u32[]{:S(2)}, u32[]{:S(2)}) collective-permute-start(f32[16,64,128]{2,1,0:T(8,128)S(1)} %get-tuple-element.97), channel_id=1, source_target_pairs={{0,4},{1,5},{2,6},{3,7},{4,8},{5,9},{6,10},{7,11},{8,12},{9,13},{1... | collective-permute-start | bytes 1572872 | tf_op jit(solution)/shard_map/ppermute | solution.py:410
  132.2 29.7 %collective-permute-start.10 = (f32[16,64,128]{2,1,0:T(8,128)S(1)}, f32[16,64,128]{2,1,0:T(8,128)S(1)}, u32[]{:S(2)}, u32[]{:S(2)}) collective-permute-start(f32[16,64,128]{2,1,0:T(8,128)S(1)} %get-tuple-element.98), channel_id=1, source_target_pairs={{0,8},{1,9},{2,10},{3,11},{4,12},{5,13},{6,14},{7,15},{8,0},{9,1},... | collective-permute-start | bytes 1572872 | tf_op jit(solution)/shard_map/ppermute | solution.py:410
  142.2 21.0 %collective-permute-start.11 = (f32[16,64,128]{2,1,0:T(8,128)S(1)}, f32[16,64,128]{2,1,0:T(8,128)S(1)}, u32[]{:S(2)}, u32[]{:S(2)}) collective-permute-start(f32[16,64,128]{2,1,0:T(8,128)S(1)} %get-tuple-element.99), channel_id=1, source_target_pairs={{0,12},{1,13},{2,14},{3,15},{4,0},{5,1},{6,2},{7,3},{8,4},{9,5},{1... | collective-permute-start | bytes 1572872 | tf_op jit(solution)/shard_map/ppermute | solution.py:410
  143.6 30.9 %collective-permute-start.31 = (f32[4,64,128]{2,1,0:T(8,128)S(1)}, f32[4,64,128]{2,1,0:T(8,128)S(1)}, u32[]{:S(2)}, u32[]{:S(2)}) collective-permute-start(f32[4,64,128]{2,1,0:T(8,128)S(1)} %get-tuple-element.133), channel_id=1, source_target_pairs={{0,16},{16,0},{32,48},{48,32},{64,80},{80,64},{96,112},{112,96},{1... | collective-permute-start | bytes 393224 | tf_op jit(solution)/shard_map/ppermute | solution.py:418
  159.1 16.3 %collective-permute-start.32 = (f32[4,64,128]{2,1,0:T(8,128)S(1)}, f32[4,64,128]{2,1,0:T(8,128)S(1)}, u32[]{:S(2)}, u32[]{:S(2)}) collective-permute-start(f32[4,64,128]{2,1,0:T(8,128)S(1)} %get-tuple-element.134), channel_id=1, source_target_pairs={{0,32},{16,48},{32,64},{48,80},{64,96},{80,112},{96,0},{112,16},{1... | collective-permute-start | bytes 393224 | tf_op jit(solution)/shard_map/ppermute | solution.py:418
  160.3 15.1 %collective-permute-start.33 = (f32[4,64,128]{2,1,0:T(8,128)S(1)}, f32[4,64,128]{2,1,0:T(8,128)S(1)}, u32[]{:S(2)}, u32[]{:S(2)}) collective-permute-start(f32[4,64,128]{2,1,0:T(8,128)S(1)} %get-tuple-element.135), channel_id=1, source_target_pairs={{0,48},{16,32},{32,80},{48,64},{64,112},{80,96},{96,16},{112,0},{1... | collective-permute-start | bytes 393224 | tf_op jit(solution)/shard_map/ppermute | solution.py:418
  (26 other events, 525.3 us)

commit v2 on v1

--- a/solution.py
+++ b/solution.py
@@ -15,11 +15,14 @@
 SIDE = 4
 CHUNKS = (128, 128)
 RELAY = (False, False)
-FAR = (1, 3, 2)
+FAR = (2, 1, 3)
+UNROLL = 4
+AHEAD = 8
 WINDOW = 256
 
 VMEM = pltpu.MemorySpace.VMEM
 MIB = 1 << 20
+FIRST_MIB = 52
 
 
 def ramp_table(length):
@@ -47,8 +50,16 @@
     )
 
 
-def bin_kernel(slot_ref, cover_ref, mon_ref, fr_ref, wt_ref, *rest, begin):
-    outs, (pixels, tiles, hold, sem, out_sem) = rest[:-5], rest[-5:]
+def bin_kernel(slot_any, cover_any, mon_any, fr_ref, wt_ref, *rest, begin):
+    outs = rest[:-9]
+    pixels, tiles, hold, slot_ref, cover_ref, mon_ref, sem, out_sem, small_sem = rest[-9:]
+    small = [
+        pltpu.make_async_copy(mon_any, mon_ref, small_sem.at[2]),
+        pltpu.make_async_copy(slot_any, slot_ref, small_sem.at[0]),
+        pltpu.make_async_copy(cover_any, cover_ref, small_sem.at[1]),
+    ]
+    for copy in small:
+        copy.start()
     groups = sem.shape[1]
     depth = pixels.shape[1] // groups
     splits = tiles.shape[0] // groups
@@ -69,33 +80,50 @@
             ),
         )
 
-    for g in range(groups):
+    for g in range(AHEAD):
         for copy in fetch(g):
             copy.start()
     me = lax.axis_index("module")
     z, x = me // SIDE, me % SIDE
+    for copy in small:
+        copy.wait()
+    flux = mon_ref[0:1, pl.ds(begin, rows)]
+    diagonal = lax.broadcasted_iota(jnp.int32, (rows, rows), 0) == lax.broadcasted_iota(
+        jnp.int32, (rows, rows), 1
+    )
+    scale = 1.0 / jnp.sum(jnp.where(diagonal, flux, 0.0), axis=1, keepdims=True)
     first = cover_ref[me, 0]
-    scale = 1.0 / mon_ref[...]
-
-    def one(g, carry):
-        for copy in fetch(g):
-            copy.wait()
-        across = pl.ds(pl.multiple_of(g * depth, depth), depth)
-        here = jnp.concatenate([tiles[g * splits + s] for s in range(splits)], axis=1)
-        bins = jnp.dot(pixels[:, across], here, preferred_element_type=jnp.float32)
-        bins = bins * scale
-        for s in range(splits):
-            slot = slot_ref[0, g * splits + s]
-            owner = (first + slot) & (SIDE * SIDE - 1)
-            turn = slot // (SIDE * SIDE)
-            away_z = (owner // SIDE - z) & (SIDE - 1)
-            away_x = (owner - x) & (SIDE - 1)
-            cut = slice(s * width, (s + 1) * width)
-            hold[0, (away_x * SIDE + away_z) * span + turn] = bins[:half, cut]
-            hold[1, (away_z * SIDE + away_x) * span + turn] = bins[half:, cut]
+
+    def one(turn_pos, carry):
+        base = turn_pos * UNROLL
+        for u in range(UNROLL):
+            for copy in fetch(base + u):
+                copy.wait()
+
+        @pl.when(base + AHEAD < groups)
+        def _():
+            for u in range(UNROLL):
+                for copy in fetch(base + AHEAD + u):
+                    copy.start()
+
+        for u in range(UNROLL):
+            g = base + u
+            across = pl.ds(pl.multiple_of(g * depth, depth), depth)
+            here = jnp.concatenate([tiles[g * splits + s] for s in range(splits)], axis=1)
+            bins = jnp.dot(pixels[:, across], here, preferred_element_type=jnp.float32)
+            bins = bins * scale
+            for s in range(splits):
+                slot = slot_ref[0, g * splits + s]
+                owner = (first + slot) & (SIDE * SIDE - 1)
+                turn = slot // (SIDE * SIDE)
+                away_z = (owner // SIDE - z) & (SIDE - 1)
+                away_x = (owner - x) & (SIDE - 1)
+                cut = slice(s * width, (s + 1) * width)
+                hold[0, (away_x * SIDE + away_z) * span + turn] = bins[:half, cut]
+                hold[1, (away_z * SIDE + away_x) * span + turn] = bins[half:, cut]
         return carry
 
-    lax.fori_loop(0, groups, one, 0)
+    lax.fori_loop(0, groups // UNROLL, one, 0)
     each = outs[0].shape[0]
     copies = [
         pltpu.make_async_copy(
@@ -109,34 +137,41 @@
         copy.wait()
 
 
-def bin_chunk(block_slot, coverage, frames, weights, monitor, begin, rows):
+def stay(value):
+    return pltpu.with_memory_space_constraint(value, pltpu.MemorySpace.HBM)
+
+
+def bin_chunk(block_slot, coverage, frames, weights, monitor, begin, rows, tag):
     pixels = frames.shape[1]
     slots, group_pixels, width = weights.shape
     groups = pixels // group_pixels
     half = rows // 2
     each = slots // SIDE
-    smem = pl.BlockSpec(memory_space=pltpu.MemorySpace.SMEM)
     anywhere = pl.BlockSpec(memory_space=pl.ANY)
     in_hbm = pl.BlockSpec(memory_space=pltpu.MemorySpace.HBM)
     return pl.pallas_call(
         functools.partial(bin_kernel, begin=begin),
         out_shape=[jax.ShapeDtypeStruct((each, half, width), jnp.float32)] * (2 * SIDE),
-        in_specs=[smem, smem, pl.BlockSpec(memory_space=VMEM), in_hbm, in_hbm],
-        out_specs=[anywhere] * (2 * SIDE),
+        in_specs=[in_hbm] * 5,
+        out_specs=[in_hbm if n % SIDE == 0 else anywhere for n in range(2 * SIDE)],
         scratch_shapes=[
             pltpu.VMEM((rows, pixels), frames.dtype),
             pltpu.VMEM(weights.shape, weights.dtype),
             pltpu.VMEM((2, slots, half, width), jnp.float32),
+            pltpu.SMEM(block_slot.shape, jnp.int32),
+            pltpu.SMEM(coverage.shape, jnp.int32),
+            pltpu.VMEM((1, monitor.size), monitor.dtype),
             pltpu.SemaphoreType.DMA((2, groups)),
             pltpu.SemaphoreType.DMA((2 * SIDE,)),
+            pltpu.SemaphoreType.DMA((3,)),
         ],
-        compiler_params=pltpu.CompilerParams(vmem_limit_bytes=(26 if begin else 55) * MIB),
+        compiler_params=pltpu.CompilerParams(vmem_limit_bytes=(26 if tag else FIRST_MIB) * MIB),
         cost_estimate=pl.CostEstimate(
             flops=2 * rows * pixels * slots // groups * width,
             bytes_accessed=2 * slots * group_pixels * width + 6 * rows * pixels,
             transcendentals=0,
         ),
-    )(block_slot, coverage, monitor[begin : begin + rows, None], frames, weights)
+    )(*(stay(v) for v in (block_slot, coverage, monitor.reshape(1, -1), frames, weights)))
 
 
 def merge_kernel(cover_ref, *rest, axis, relay):
@@ -333,7 +368,7 @@
                 (1, strips, angles, WINDOW, cols), lambda i, start: (i, 0, 0, 0, 0)
             ),
         ),
-        compiler_params=pltpu.CompilerParams(vmem_limit_bytes=10 * MIB),
+        compiler_params=pltpu.CompilerParams(vmem_limit_bytes=48 * MIB),
         cost_estimate=pl.CostEstimate(
             flops=5 * pairs * count * WINDOW * cols,
             bytes_accessed=2 * pairs * count * WINDOW * cols,
@@ -351,7 +386,12 @@
         across = pl.ds(pl.multiple_of(pair * 2 * line, 2 * line), 2 * line)
         return pltpu.make_async_copy(done.at[:, across], out_ref.at[:, across], out_sem.at[pair])
 
-    def one(pair, carry):
+    def one(step, carry):
+        for u in range(4):
+            project(step * 4 + u)
+        return carry
+
+    def project(pair):
         for strip in range(strips):
             total = None
             for a in range(angles):
@@ -367,9 +407,8 @@
                 to = pl.multiple_of(pair * 2 * line + r * line + strip * cols, 128)
                 done[:, pl.ds(to, cols)] = total[:, r * cols : (r + 1) * cols]
         put(pair).start()
-        return carry
-
-    lax.fori_loop(0, pairs, one, 0)
+
+    lax.fori_loop(0, pairs // 4, one, 0)
     for pair in range(pairs):
         put(pair).wait()
 
@@ -454,8 +493,8 @@
 
     begins = [sum(CHUNKS[:c]) for c in range(len(CHUNKS))]
     sent = [
-        bin_chunk(block_slot, coverage, frames, weights, monitor, begin, rows)
-        for begin, rows in zip(begins, CHUNKS)
+        bin_chunk(block_slot, coverage, frames, weights, monitor, begin, rows, c)
+        for c, (begin, rows) in enumerate(zip(begins, CHUNKS))
     ]
     filt = None
     arrived = first_leg(sent[0])
@@ -465,15 +504,7 @@
         here = arrived
         last = c + 1 == len(CHUNKS)
         if not last:
-            extra = (ramp, tables) if c == 0 else ()
-            held = []
-            for side in range(2):
-                ready = sent[c + 1][side * SIDE : (side + 1) * SIDE]
-                ready, here[side], extra = lax.optimization_barrier((ready, here[side], extra))
-                held += ready
-            if c == 0:
-                ramp, tables = extra
-            arrived = first_leg(held)
+            arrived = first_leg(sent[c + 1])
         lines = second_leg(here, RELAY[c])
         filt = ramp_chunk(ramp, lines, filt, begin, last, angles)
     slices = back_project(start, filt, tables)

time: 206 us -> 204 us (level)
  starting transfers between devices: 71.2 us -> 64.1 us
  local copies, waits for them, and re-layouts: 10.6 us -> 16.7 us
  waiting for transfers between devices: 74.9 us -> 70.9 us
  Pallas kernels: 47.3 us -> 50.5 us
    ppermute x14, starting transfers between devices: 41.7 us -> 26.2 us  [swap(): return lax.ppermute(array, 'frame', pairs)]
    ppermute x14, waiting for transfers between devices: 9.45 us -> 0.29 us  [swap(): return lax.ppermute(array, 'frame', pairs)]
    ppermute x24, starting transfers between devices: 29.5 us -> 37.9 us  [shift(): return lax.ppermute(array, 'module', pairs)]
    unnamed x25 -> x35, local copies, waits for them, and re-layouts: 8.63 us -> 15 us
    ppermute x24, waiting for transfers between devices: 65.4 us -> 70.6 us  [shift(): return lax.ppermute(array, 'module', pairs)]
    pallas_call x1, Pallas kernels: 6.73 us -> 9.86 us  [make_tables(): pl.pallas_call(table_kernel, name='tables', out_shape=jax.ShapeDtypeStruc...]
    pallas_call x2, Pallas kernels: 20.3 us -> 17.8 us  [bin_chunk(): pl.pallas_call(functools.partial(bin_kernel, begin=begin), out_shape=[jax...]
    pallas_call x2, Pallas kernels: 0.49 us -> 2.82 us  [join(): pl.pallas_call(functools.partial(join_kernel, relay=relay), out_shape=[ja...]
  transfers between devices with their start and end apart: 38 -> 38, of which waited for: 13 -> 11; matrix products, arithmetic and copies ran while one was open for 1% -> 1% of each run, Pallas kernels for 13% -> 16%
where the time goes in v2:
time: 204 us
  waiting for transfers between devices  70.9 us (35%)
  starting transfers between devices  64.1 us (31%)
  Pallas kernels  50.5 us (25%)
  local copies, waits for them, and re-layouts  16.7 us (8%)
    ppermute x24, waiting for transfers between devices, shift(): return lax.ppermute(array, 'module', pairs)  70.6 us
    ppermute x24, starting transfers between devices, shift(): return lax.ppermute(array, 'module', pairs)  37.9 us
    ppermute x14, starting transfers between devices, swap(): return lax.ppermute(array, 'frame', pairs)  26.2 us
    pallas_call x2, Pallas kernels, bin_chunk(): pl.pallas_call(functools.partial(bin_kernel, begin=begin), out_shape=[jax...  17.8 us
    unnamed x35, local copies, waits for them, and re-layouts  15 us
    pallas_call x4, Pallas kernels, merge(): pl.pallas_call(functools.partial(merge_kernel, axis=axis, relay=relay), o...  10.7 us
    pallas_call x1, Pallas kernels, make_tables(): pl.pallas_call(table_kernel, name='tables', out_shape=jax.ShapeDtypeStruc...  9.86 us
    pallas_call x1, Pallas kernels, back_project(): pl.pallas_call(functools.partial(back_kernel, scale=math.pi / angles), na...  7.3 us
  transfers between devices with their start and end apart: 38, of which 11 were waited for; matrix products, arithmetic and copies ran while one was open for 1% of the time, Pallas kernels for 16%

profile of v2, /device:TPU:1, one launch (start us, length us, event | category | flops | bytes accessed | tf_op | source)
XLA Modules:
  0.0 203.8 jit_solution(13412399981726543491)
XLA Ops:
  0.0 9.8 %shard_map.68 = (f32[24,64,128]{2,1,0:T(8,128)S(1)}, f32[24,64,128]{2,1,0:T(8,128)S(1)}, f32[24,64,128]{2,1,0:T(8,128)}, f32[24,64,128]{2,1,0:T(8,128)}, f32[24,...) custom-call(s32[1,96]{1,0:T(1,128)} %slot_any.3, ...), custom_call_target="tpu_custom_call" | custom-call | flops 1610612736 | bytes 22020096 | tf_op jit(solution)/shard_map/pallas_call | solution.py:152
  17.2 3.3 %collective-permute-start.26 = (f32[24,64,128]{2,1,0:T(8,128)}, f32[24,64,128]{2,1,0:T(8,128)S(1)}, u32[]{:S(2)}, u32[]{:S(2)}) collective-permute-start(f32[24,64,128]{2,1,0:T(8,128)} %get-tuple-element.87), channel_id=1, source_target_pairs={{0,8},{1,9},{2,10},{3,11},{4,12},{5,13},{6,14},{7,15},{8,0},{9,1},... | collective-permute-start | bytes 2359304 | tf_op jit(solution)/shard_map/ppermute | solution.py:449
  20.5 8.0 %shard_map.64 = (f32[24,64,128]{2,1,0:T(8,128)S(1)}, f32[24,64,128]{2,1,0:T(8,128)S(1)}, f32[24,64,128]{2,1,0:T(8,128)S(1)}, f32[24,64,128]{2,1,0:T(8,128)S(1)},...) custom-call(s32[1,96]{1,0:T(1,128)} %slot_any.3, ...), custom_call_target="tpu_custom_call" | custom-call | flops 1610612736 | bytes 22020096 | tf_op jit(solution)/shard_map/pallas_call | solution.py:152
  30.1 4.0 %collective-permute-start.27 = (f32[24,64,128]{2,1,0:T(8,128)S(1)}, f32[24,64,128]{2,1,0:T(8,128)S(1)}, u32[]{:S(2)}, u32[]{:S(2)}) collective-permute-start(f32[24,64,128]{2,1,0:T(8,128)S(1)} %copy-done.15), channel_id=1, source_target_pairs={{0,12},{1,13},{2,14},{3,15},{4,0},{5,1},{6,2},{7,3},{8,4},{9,5},{1... | collective-permute-start | bytes 2359304 | tf_op jit(solution)/shard_map/ppermute | solution.py:449
  34.1 14.1 %collective-permute-done.20.rest_2_ = f32[24,64,128]{2,1,0:T(8,128)S(1)} collective-permute-done((f32[24,64,128]{2,1,0:T(8,128)}, f32[24,64,128]{2,1,0:T(8,128)S(1)}, u32[]{:S(2)}, u32[]{:S(2)}) %collective-permute-start.20) | collective-permute-done | bytes 786464 | tf_op jit(solution)/shard_map/ppermute | solution.py:449
  53.9 3.3 %collective-permute-start.7 = (f32[24,64,128]{2,1,0:T(8,128)S(1)}, f32[24,64,128]{2,1,0:T(8,128)S(1)}, u32[]{:S(2)}, u32[]{:S(2)}) collective-permute-start(f32[24,64,128]{2,1,0:T(8,128)S(1)} %get-tuple-element.63), channel_id=1, source_target_pairs={{0,8},{1,9},{2,10},{3,11},{4,12},{5,13},{6,14},{7,15},{8,0},{9,1},... | collective-permute-start | bytes 2359304 | tf_op jit(solution)/shard_map/ppermute | solution.py:449
  57.1 26.7 %collective-permute-done.rest_1_ = f32[24,64,128]{2,1,0:T(8,128)S(1)} collective-permute-done((f32[24,64,128]{2,1,0:T(8,128)S(1)}, f32[24,64,128]{2,1,0:T(8,128)S(1)}, u32[]{:S(2)}, u32[]{:S(2)}) %collective-permute-start) | collective-permute-done | bytes 786464 | tf_op jit(solution)/shard_map/ppermute | solution.py:449
  83.8 3.8 %collective-permute-start.8 = (f32[24,64,128]{2,1,0:T(8,128)S(1)}, f32[24,64,128]{2,1,0:T(8,128)S(1)}, u32[]{:S(2)}, u32[]{:S(2)}) collective-permute-start(f32[24,64,128]{2,1,0:T(8,128)S(1)} %get-tuple-element.64), channel_id=1, source_target_pairs={{0,12},{1,13},{2,14},{3,15},{4,0},{5,1},{6,2},{7,3},{8,4},{9,5},{1... | collective-permute-start | bytes 2359304 | tf_op jit(solution)/shard_map/ppermute | solution.py:449
  94.7 9.1 %collective-permute-done.8.rest_3_ = f32[24,64,128]{2,1,0:T(8,128)S(1)} collective-permute-done((f32[24,64,128]{2,1,0:T(8,128)S(1)}, f32[24,64,128]{2,1,0:T(8,128)S(1)}, u32[]{:S(2)}, u32[]{:S(2)}) %collective-permute-start.8) | collective-permute-done | bytes 786464 | tf_op jit(solution)/shard_map/ppermute | solution.py:449
  103.9 3.1 %shard_map.65 = (f32[16,64,128]{2,1,0:T(8,128)S(1)}, f32[16,64,128]{2,1,0:T(8,128)S(1)}, f32[16,64,128]{2,1,0:T(8,128)}, f32[16,64,128]{2,1,0:T(8,128)}) custom-call(s32[16,96]{1,0:T(8,128)S(1)} %copy-done.12, f32[24,64,128]{2,1,0:T(8,128)S(1)} %get-tuple-element.53.rest_0_, f32[24,64,128]{2,1,0:T(8,128)S(1)} %collective-permute-done.rest_1_, ...), custom_call_target="tpu_custom_call" | custom-call | flops 2097152 | bytes 5242880 | tf_op jit(solution)/shard_map/pallas_call | solution.py:237
  107.0 4.7 %collective-permute-done.23.refs_2_ = f32[16,64,128]{2,1,0:T(8,128)S(1)} collective-permute-done((f32[16,64,128]{2,1,0:T(8,128)S(1)}, f32[16,64,128]{2,1,0:T(8,128)S(1)}, u32[]{:S(2)}, u32[]{:S(2)}) %collective-permute-start.23) | collective-permute-done | bytes 524320 | tf_op jit(solution)/shard_map/ppermute | solution.py:449
  111.7 3.1 %collective-permute-start.3 = (f32[16,64,128]{2,1,0:T(8,128)S(1)}, f32[16,64,128]{2,1,0:T(8,128)S(1)}, u32[]{:S(2)}, u32[]{:S(2)}) collective-permute-start(f32[16,64,128]{2,1,0:T(8,128)S(1)} %get-tuple-element.58), channel_id=1, source_target_pairs={{0,4},{1,5},{2,6},{3,7},{4,8},{5,9},{6,10},{7,11},{8,12},{9,13},{1... | collective-permute-start | bytes 1572872 | tf_op jit(solution)/shard_map/ppermute | solution.py:449
  114.8 3.3 %shard_map.66 = (f32[16,64,128]{2,1,0:T(8,128)S(1)}, f32[16,64,128]{2,1,0:T(8,128)}, f32[16,64,128]{2,1,0:T(8,128)}, f32[16,64,128]{2,1,0:T(8,128)}) custom-call(s32[16,96]{1,0:T(8,128)S(1)} %copy-done.12, f32[24,64,128]{2,1,0:T(8,128)S(1)} %get-tuple-element.61.rest_0_, f32[24,64,128]{2,1,0:T(8,128)S(1)} %collective-permute-done.6.rest_1_, ...), custom_call_target="tpu_custom_call" | custom-call | flops 2097152 | bytes 5242880 | tf_op jit(solution)/shard_map/pallas_call | solution.py:237
  118.9 5.6 %collective-permute-done.24.refs_3_ = f32[16,64,128]{2,1,0:T(8,128)S(1)} collective-permute-done((f32[16,64,128]{2,1,0:T(8,128)S(1)}, f32[16,64,128]{2,1,0:T(8,128)S(1)}, u32[]{:S(2)}, u32[]{:S(2)}) %collective-permute-start.24) | collective-permute-done | bytes 524320 | tf_op jit(solution)/shard_map/ppermute | solution.py:449
  131.3 2.9 %collective-permute-start.11 = (f32[16,64,128]{2,1,0:T(8,128)}, f32[16,64,128]{2,1,0:T(8,128)}, u32[]{:S(2)}, u32[]{:S(2)}) collective-permute-start(f32[16,64,128]{2,1,0:T(8,128)} %get-tuple-element.68), channel_id=1, source_target_pairs={{0,3},{1,0},{2,1},{3,2},{4,7},{5,4},{6,5},{7,6},{8,11},{9,8},{10,9... | collective-permute-start | bytes 1572872 | tf_op jit(solution)/shard_map/ppermute | solution.py:449
  141.1 6.9 %collective-permute-start.31 = (f32[4,64,128]{2,1,0:T(8,128)S(1)}, f32[4,64,128]{2,1,0:T(8,128)S(1)}, u32[]{:S(2)}, u32[]{:S(2)}) collective-permute-start(f32[4,64,128]{2,1,0:T(8,128)S(1)} %get-tuple-element.94), channel_id=1, source_target_pairs={{0,16},{16,0},{32,48},{48,32},{64,80},{80,64},{96,112},{112,96},{1... | collective-permute-start | bytes 393224 | tf_op jit(solution)/shard_map/ppermute | solution.py:457
  148.0 4.2 %collective-permute-done.5.refs_3_ = f32[16,64,128]{2,1,0:T(8,128)} collective-permute-done((f32[16,64,128]{2,1,0:T(8,128)}, f32[16,64,128]{2,1,0:T(8,128)}, u32[]{:S(2)}, u32[]{:S(2)}) %collective-permute-start.5) | collective-permute-done | bytes 524320 | tf_op jit(solution)/shard_map/ppermute | solution.py:449
  155.9 2.8 %collective-permute-start.33 = (f32[4,64,128]{2,1,0:T(8,128)S(1)}, f32[4,64,128]{2,1,0:T(8,128)S(1)}, u32[]{:S(2)}, u32[]{:S(2)}) collective-permute-start(f32[4,64,128]{2,1,0:T(8,128)S(1)} %get-tuple-element.96), channel_id=1, source_target_pairs={{0,48},{16,32},{32,80},{48,64},{64,112},{80,96},{96,16},{112,0},{1... | collective-permute-start | bytes 393224 | tf_op jit(solution)/shard_map/ppermute | solution.py:457
  158.7 2.6 %collective-permute-start.34 = (f32[4,64,128]{2,1,0:T(8,128)S(1)}, f32[4,64,128]{2,1,0:T(8,128)S(1)}, u32[]{:S(2)}, u32[]{:S(2)}) collective-permute-start(f32[4,64,128]{2,1,0:T(8,128)S(1)} %get-tuple-element.97), channel_id=1, source_target_pairs={{0,64},{16,80},{32,96},{48,112},{64,0},{80,16},{96,32},{112,48},{1... | collective-permute-start | bytes 393224 | tf_op jit(solution)/shard_map/ppermute | solution.py:457
  170.5 3.6 %collective-permute-start.15 = (f32[4,64,128]{2,1,0:T(8,128)}, f32[4,64,128]{2,1,0:T(8,128)S(1)}, u32[]{:S(2)}, u32[]{:S(2)}) collective-permute-start(f32[4,64,128]{2,1,0:T(8,128)} %get-tuple-element.73), channel_id=1, source_target_pairs={{0,64},{16,80},{32,96},{48,112},{64,0},{80,16},{96,32},{112,48},{1... | collective-permute-start | bytes 393224 | tf_op jit(solution)/shard_map/ppermute | solution.py:457
  175.4 3.0 %collective-permute-start.17 = (f32[4,64,128]{2,1,0:T(8,128)}, f32[4,64,128]{2,1,0:T(8,128)S(1)}, u32[]{:S(2)}, u32[]{:S(2)}) collective-permute-start(f32[4,64,128]{2,1,0:T(8,128)} %get-tuple-element.75), channel_id=1, source_target_pairs={{0,96},{16,112},{32,0},{48,16},{64,32},{80,48},{96,64},{112,80},{1... | collective-permute-start | bytes 393224 | tf_op jit(solution)/shard_map/ppermute | solution.py:457
  178.6 9.9 %tables.1 = bf16[8,4,4,256,256]{4,3,2,1,0:T(8,128)(2,1)} custom-call(s32[8,16]{1,0:T(8,128)S(1)} %copy.16.start_ref, f32[8,16,256]{2,1,0:T(8,128)S(1)} %add_add_fusion.spot_ref), custom_call_target="tpu_custom_call" | custom-call | flops 41943040 | bytes 16777216 | tf_op jit(solution)/shard_map/tables/pallas_call | solution.py:359
  190.6 5.8 %copy-done = bf16[8,4,4,256,256]{4,3,2,1,0:T(8,128)(2,1)S(1)} copy-done((bf16[8,4,4,256,256]{4,3,2,1,0:T(8,128)(2,1)S(1)}, bf16[8,4,4,256,256]{4,3,2,1,0:T(8,128)(2,1)}, u32[]{:S(2)}) %copy-start) | copy-done | bytes 16777240
  196.3 7.3 %back.1 = bf16[256,8192]{1,0:T(8,128)(2,1)} custom-call(s32[8,16]{1,0:T(8,128)S(1)} %copy.16.start_ref, bf16[4,256,512]{2,1,0:T(8,128)(2,1)S(1)} %shard_map.73.filt_ref, bf16[8,4,4,256,256]{4,3,2,1,0:T(8,128)(2,1)S(1)} %copy-done), custom_call_target="tpu_custom_call" | custom-call | flops 4294967296 | bytes 20971520 | tf_op jit(solution)/shard_map/back/pallas_call | solution.py:420
  (113 shorter events, 52.5 us)
Async XLA Ops:
  9.8 20.2 %collective-permute-start.19 = (f32[24,64,128]{2,1,0:T(8,128)S(1)}, f32[24,64,128]{2,1,0:T(8,128)S(1)}, u32[]{:S(2)}, u32[]{:S(2)}) collective-permute-start(f32[24,64,128]{2,1,0:T(8,128)S(1)} %get-tuple-element.78), channel_id=1, source_target_pairs={{0,1},{1,2},{2,3},{3,0},{4,5},{5,6},{6,7},{7,4},{8,9},{9,10},{10,1... | collective-permute-start | bytes 2359304 | tf_op jit(solution)/shard_map/ppermute | solution.py:449
  11.9 36.3 %collective-permute-start.20 = (f32[24,64,128]{2,1,0:T(8,128)}, f32[24,64,128]{2,1,0:T(8,128)S(1)}, u32[]{:S(2)}, u32[]{:S(2)}) collective-permute-start(f32[24,64,128]{2,1,0:T(8,128)} %get-tuple-element.79), channel_id=1, source_target_pairs={{0,2},{1,3},{2,0},{3,1},{4,6},{5,7},{6,4},{7,5},{8,10},{9,11},{10,... | collective-permute-start | bytes 2359304 | tf_op jit(solution)/shard_map/ppermute | solution.py:449
  14.4 33.8 %collective-permute-start.21 = (f32[24,64,128]{2,1,0:T(8,128)}, f32[24,64,128]{2,1,0:T(8,128)S(1)}, u32[]{:S(2)}, u32[]{:S(2)}) collective-permute-start(f32[24,64,128]{2,1,0:T(8,128)} %get-tuple-element.80), channel_id=1, source_target_pairs={{0,3},{1,0},{2,1},{3,2},{4,7},{5,4},{6,5},{7,6},{8,11},{9,8},{10,9... | collective-permute-start | bytes 2359304 | tf_op jit(solution)/shard_map/ppermute | solution.py:449
  15.5 35.0 %collective-permute-start.25 = (f32[24,64,128]{2,1,0:T(8,128)}, f32[24,64,128]{2,1,0:T(8,128)S(1)}, u32[]{:S(2)}, u32[]{:S(2)}) collective-permute-start(f32[24,64,128]{2,1,0:T(8,128)} %get-tuple-element.86), channel_id=1, source_target_pairs={{0,4},{1,5},{2,6},{3,7},{4,8},{5,9},{6,10},{7,11},{8,12},{9,13},{1... | collective-permute-start | bytes 2359304 | tf_op jit(solution)/shard_map/ppermute | solution.py:449
  17.2 36.5 %collective-permute-start.26 = (f32[24,64,128]{2,1,0:T(8,128)}, f32[24,64,128]{2,1,0:T(8,128)S(1)}, u32[]{:S(2)}, u32[]{:S(2)}) collective-permute-start(f32[24,64,128]{2,1,0:T(8,128)} %get-tuple-element.87), channel_id=1, source_target_pairs={{0,8},{1,9},{2,10},{3,11},{4,12},{5,13},{6,14},{7,15},{8,0},{9,1},... | collective-permute-start | bytes 2359304 | tf_op jit(solution)/shard_map/ppermute | solution.py:449
  30.1 23.8 %collective-permute-start.27 = (f32[24,64,128]{2,1,0:T(8,128)S(1)}, f32[24,64,128]{2,1,0:T(8,128)S(1)}, u32[]{:S(2)}, u32[]{:S(2)}) collective-permute-start(f32[24,64,128]{2,1,0:T(8,128)S(1)} %copy-done.15), channel_id=1, source_target_pairs={{0,12},{1,13},{2,14},{3,15},{4,0},{5,1},{6,2},{7,3},{8,4},{9,5},{1... | collective-permute-start | bytes 2359304 | tf_op jit(solution)/shard_map/ppermute | solution.py:449
  48.2 35.6 %collective-permute-start = (f32[24,64,128]{2,1,0:T(8,128)S(1)}, f32[24,64,128]{2,1,0:T(8,128)S(1)}, u32[]{:S(2)}, u32[]{:S(2)}) collective-permute-start(f32[24,64,128]{2,1,0:T(8,128)S(1)} %get-tuple-element.54), channel_id=1, source_target_pairs={{0,1},{1,2},{2,3},{3,0},{4,5},{5,6},{6,7},{7,4},{8,9},{9,10},{10,1... | collective-permute-start | bytes 2359304 | tf_op jit(solution)/shard_map/ppermute | solution.py:449
  48.2 41.5 %collective-permute-start.1 = (f32[24,64,128]{2,1,0:T(8,128)S(1)}, f32[24,64,128]{2,1,0:T(8,128)S(1)}, u32[]{:S(2)}, u32[]{:S(2)}) collective-permute-start(f32[24,64,128]{2,1,0:T(8,128)S(1)} %get-tuple-element.55), channel_id=1, source_target_pairs={{0,2},{1,3},{2,0},{3,1},{4,6},{5,7},{6,4},{7,5},{8,10},{9,11},{10,... | collective-permute-start | bytes 2359304 | tf_op jit(solution)/shard_map/ppermute | solution.py:449
  50.5 39.3 %collective-permute-start.2 = (f32[24,64,128]{2,1,0:T(8,128)S(1)}, f32[24,64,128]{2,1,0:T(8,128)S(1)}, u32[]{:S(2)}, u32[]{:S(2)}) collective-permute-start(f32[24,64,128]{2,1,0:T(8,128)S(1)} %get-tuple-element.56), channel_id=1, source_target_pairs={{0,3},{1,0},{2,1},{3,2},{4,7},{5,4},{6,5},{7,6},{8,11},{9,8},{10,9... | collective-permute-start | bytes 2359304 | tf_op jit(solution)/shard_map/ppermute | solution.py:449
  53.6 39.6 %collective-permute-start.6 = (f32[24,64,128]{2,1,0:T(8,128)S(1)}, f32[24,64,128]{2,1,0:T(8,128)S(1)}, u32[]{:S(2)}, u32[]{:S(2)}) collective-permute-start(f32[24,64,128]{2,1,0:T(8,128)S(1)} %get-tuple-element.62), channel_id=1, source_target_pairs={{0,4},{1,5},{2,6},{3,7},{4,8},{5,9},{6,10},{7,11},{8,12},{9,13},{1... | collective-permute-start | bytes 2359304 | tf_op jit(solution)/shard_map/ppermute | solution.py:449
  53.9 40.8 %collective-permute-start.7 = (f32[24,64,128]{2,1,0:T(8,128)S(1)}, f32[24,64,128]{2,1,0:T(8,128)S(1)}, u32[]{:S(2)}, u32[]{:S(2)}) collective-permute-start(f32[24,64,128]{2,1,0:T(8,128)S(1)} %get-tuple-element.63), channel_id=1, source_target_pairs={{0,8},{1,9},{2,10},{3,11},{4,12},{5,13},{6,14},{7,15},{8,0},{9,1},... | collective-permute-start | bytes 2359304 | tf_op jit(solution)/shard_map/ppermute | solution.py:449
  83.8 20.0 %collective-permute-start.8 = (f32[24,64,128]{2,1,0:T(8,128)S(1)}, f32[24,64,128]{2,1,0:T(8,128)S(1)}, u32[]{:S(2)}, u32[]{:S(2)}) collective-permute-start(f32[24,64,128]{2,1,0:T(8,128)S(1)} %get-tuple-element.64), channel_id=1, source_target_pairs={{0,12},{1,13},{2,14},{3,15},{4,0},{5,1},{6,2},{7,3},{8,4},{9,5},{1... | collective-permute-start | bytes 2359304 | tf_op jit(solution)/shard_map/ppermute | solution.py:449
  89.8 21.9 %collective-permute-start.23 = (f32[16,64,128]{2,1,0:T(8,128)S(1)}, f32[16,64,128]{2,1,0:T(8,128)S(1)}, u32[]{:S(2)}, u32[]{:S(2)}) collective-permute-start(f32[16,64,128]{2,1,0:T(8,128)S(1)} %get-tuple-element.83), channel_id=1, source_target_pairs={{0,8},{1,9},{2,10},{3,11},{4,12},{5,13},{6,14},{7,15},{8,0},{9,1},... | collective-permute-start | bytes 1572872 | tf_op jit(solution)/shard_map/ppermute | solution.py:449
  93.2 31.3 %collective-permute-start.24 = (f32[16,64,128]{2,1,0:T(8,128)S(1)}, f32[16,64,128]{2,1,0:T(8,128)S(1)}, u32[]{:S(2)}, u32[]{:S(2)}) collective-permute-start(f32[16,64,128]{2,1,0:T(8,128)S(1)} %get-tuple-element.84), channel_id=1, source_target_pairs={{0,12},{1,13},{2,14},{3,15},{4,0},{5,1},{6,2},{7,3},{8,4},{9,5},{1... | collective-permute-start | bytes 1572872 | tf_op jit(solution)/shard_map/ppermute | solution.py:449
  94.7 32.7 %collective-permute-start.28 = (f32[16,64,128]{2,1,0:T(8,128)S(1)}, f32[16,64,128]{2,1,0:T(8,128)S(1)}, u32[]{:S(2)}, u32[]{:S(2)}) collective-permute-start(f32[16,64,128]{2,1,0:T(8,128)S(1)} %get-tuple-element.90), channel_id=1, source_target_pairs={{0,1},{1,2},{2,3},{3,0},{4,5},{5,6},{6,7},{7,4},{8,9},{9,10},{10,1... | collective-permute-start | bytes 1572872 | tf_op jit(solution)/shard_map/ppermute | solution.py:449
  103.8 25.8 %collective-permute-start.29 = (f32[16,64,128]{2,1,0:T(8,128)S(1)}, f32[16,64,128]{2,1,0:T(8,128)S(1)}, u32[]{:S(2)}, u32[]{:S(2)}) collective-permute-start(f32[16,64,128]{2,1,0:T(8,128)S(1)} %get-tuple-element.91), channel_id=1, source_target_pairs={{0,2},{1,3},{2,0},{3,1},{4,6},{5,7},{6,4},{7,5},{8,10},{9,11},{10,... | collective-permute-start | bytes 1572872 | tf_op jit(solution)/shard_map/ppermute | solution.py:449
  103.8 26.6 %collective-permute-start.30 = (f32[16,64,128]{2,1,0:T(8,128)S(1)}, f32[16,64,128]{2,1,0:T(8,128)S(1)}, u32[]{:S(2)}, u32[]{:S(2)}) collective-permute-start(f32[16,64,128]{2,1,0:T(8,128)S(1)} %get-tuple-element.92), channel_id=1, source_target_pairs={{0,3},{1,0},{2,1},{3,2},{4,7},{5,4},{6,5},{7,6},{8,11},{9,8},{10,9... | collective-permute-start | bytes 1572872 | tf_op jit(solution)/shard_map/ppermute | solution.py:449
  111.7 19.6 %collective-permute-start.3 = (f32[16,64,128]{2,1,0:T(8,128)S(1)}, f32[16,64,128]{2,1,0:T(8,128)S(1)}, u32[]{:S(2)}, u32[]{:S(2)}) collective-permute-start(f32[16,64,128]{2,1,0:T(8,128)S(1)} %get-tuple-element.58), channel_id=1, source_target_pairs={{0,4},{1,5},{2,6},{3,7},{4,8},{5,9},{6,10},{7,11},{8,12},{9,13},{1... | collective-permute-start | bytes 1572872 | tf_op jit(solution)/shard_map/ppermute | solution.py:449
  128.2 24.0 %collective-permute-start.5 = (f32[16,64,128]{2,1,0:T(8,128)}, f32[16,64,128]{2,1,0:T(8,128)}, u32[]{:S(2)}, u32[]{:S(2)}) collective-permute-start(f32[16,64,128]{2,1,0:T(8,128)} %get-tuple-element.60), channel_id=1, source_target_pairs={{0,12},{1,13},{2,14},{3,15},{4,0},{5,1},{6,2},{7,3},{8,4},{9,5},{1... | collective-permute-start | bytes 1572872 | tf_op jit(solution)/shard_map/ppermute | solution.py:449
  130.4 25.5 %collective-permute-start.9 = (f32[16,64,128]{2,1,0:T(8,128)}, f32[16,64,128]{2,1,0:T(8,128)}, u32[]{:S(2)}, u32[]{:S(2)}) collective-permute-start(f32[16,64,128]{2,1,0:T(8,128)} %get-tuple-element.66), channel_id=1, source_target_pairs={{0,1},{1,2},{2,3},{3,0},{4,5},{5,6},{6,7},{7,4},{8,9},{9,10},{10,1... | collective-permute-start | bytes 1572872 | tf_op jit(solution)/shard_map/ppermute | solution.py:449
  131.2 27.5 %collective-permute-start.10 = (f32[16,64,128]{2,1,0:T(8,128)}, f32[16,64,128]{2,1,0:T(8,128)}, u32[]{:S(2)}, u32[]{:S(2)}) collective-permute-start(f32[16,64,128]{2,1,0:T(8,128)} %get-tuple-element.67), channel_id=1, source_target_pairs={{0,2},{1,3},{2,0},{3,1},{4,6},{5,7},{6,4},{7,5},{8,10},{9,11},{10,... | collective-permute-start | bytes 1572872 | tf_op jit(solution)/shard_map/ppermute | solution.py:449
  131.3 30.6 %collective-permute-start.11 = (f32[16,64,128]{2,1,0:T(8,128)}, f32[16,64,128]{2,1,0:T(8,128)}, u32[]{:S(2)}, u32[]{:S(2)}) collective-permute-start(f32[16,64,128]{2,1,0:T(8,128)} %get-tuple-element.68), channel_id=1, source_target_pairs={{0,3},{1,0},{2,1},{3,2},{4,7},{5,4},{6,5},{7,6},{8,11},{9,8},{10,9... | collective-permute-start | bytes 1572872 | tf_op jit(solution)/shard_map/ppermute | solution.py:449
  141.1 24.5 %collective-permute-start.31 = (f32[4,64,128]{2,1,0:T(8,128)S(1)}, f32[4,64,128]{2,1,0:T(8,128)S(1)}, u32[]{:S(2)}, u32[]{:S(2)}) collective-permute-start(f32[4,64,128]{2,1,0:T(8,128)S(1)} %get-tuple-element.94), channel_id=1, source_target_pairs={{0,16},{16,0},{32,48},{48,32},{64,80},{80,64},{96,112},{112,96},{1... | collective-permute-start | bytes 393224 | tf_op jit(solution)/shard_map/ppermute | solution.py:457
  169.6 19.9 %collective-permute-start.14 = (f32[4,64,128]{2,1,0:T(8,128)}, f32[4,64,128]{2,1,0:T(8,128)S(1)}, u32[]{:S(2)}, u32[]{:S(2)}) collective-permute-start(f32[4,64,128]{2,1,0:T(8,128)} %get-tuple-element.72), channel_id=1, source_target_pairs={{0,48},{16,32},{32,80},{48,64},{64,112},{80,96},{96,16},{112,0},{1... | collective-permute-start | bytes 393224 | tf_op jit(solution)/shard_map/ppermute | solution.py:457
  (31 other events, 489.0 us)

commit v3 on v2

--- a/solution.py
+++ b/solution.py
@@ -13,7 +13,7 @@
 ROWS = 16
 NTILE = 256
 SIDE = 4
-CHUNKS = (128, 128)
+CHUNKS = (160, 96)
 RELAY = (False, False)
 FAR = (2, 1, 3)
 UNROLL = 4
@@ -22,7 +22,7 @@
 
 VMEM = pltpu.MemorySpace.VMEM
 MIB = 1 << 20
-FIRST_MIB = 52
+FIRST_MIB = 50
 
 
 def ramp_table(length):
@@ -368,7 +368,7 @@
                 (1, strips, angles, WINDOW, cols), lambda i, start: (i, 0, 0, 0, 0)
             ),
         ),
-        compiler_params=pltpu.CompilerParams(vmem_limit_bytes=48 * MIB),
+        compiler_params=pltpu.CompilerParams(vmem_limit_bytes=40 * MIB),
         cost_estimate=pl.CostEstimate(
             flops=5 * pairs * count * WINDOW * cols,
             bytes_accessed=2 * pairs * count * WINDOW * cols,

time: 204 us -> 282 us (1.38); the launches traced: 204 us -> 277 us
  waiting for transfers between devices: 70.9 us -> 162 us
  starting transfers between devices: 64.1 us -> 52.5 us
  local copies, waits for them, and re-layouts: 16.7 us -> 9 us
    ppermute x24, waiting for transfers between devices: 70.6 us -> 155 us  [shift(): return lax.ppermute(array, 'module', pairs)]
    unnamed x35 -> x19, local copies, waits for them, and re-layouts: 15 us -> 5.81 us
    ppermute x24, starting transfers between devices: 37.9 us -> 30.4 us  [shift(): return lax.ppermute(array, 'module', pairs)]
    ppermute x14, waiting for transfers between devices: 0.29 us -> 7.09 us  [swap(): return lax.ppermute(array, 'frame', pairs)]
    ppermute x14, starting transfers between devices: 26.2 us -> 22.1 us  [swap(): return lax.ppermute(array, 'frame', pairs)]
  transfers between devices with their start and end apart: 38 -> 38, of which waited for: 11 -> 13; matrix products, arithmetic and copies ran while one was open for 1% -> 2% of each run, Pallas kernels for 16% -> 12%
where the time goes in v3:
time: 282 us; the launch traced here: 277 us
  waiting for transfers between devices  162 us (57%)
  starting transfers between devices  52.5 us (19%)
  Pallas kernels  49.8 us (18%)
  local copies, waits for them, and re-layouts  9 us (3%)
    ppermute x24, waiting for transfers between devices, shift(): return lax.ppermute(array, 'module', pairs)  155 us
    ppermute x24, starting transfers between devices, shift(): return lax.ppermute(array, 'module', pairs)  30.4 us
    ppermute x14, starting transfers between devices, swap(): return lax.ppermute(array, 'frame', pairs)  22.1 us
    pallas_call x2, Pallas kernels, bin_chunk(): pl.pallas_call(functools.partial(bin_kernel, begin=begin), out_shape=[jax...  19.7 us
    pallas_call x1, Pallas kernels, make_tables(): pl.pallas_call(table_kernel, name='tables', out_shape=jax.ShapeDtypeStruc...  9.87 us
    pallas_call x4, Pallas kernels, merge(): pl.pallas_call(functools.partial(merge_kernel, axis=axis, relay=relay), o...  8.32 us
    pallas_call x1, Pallas kernels, back_project(): pl.pallas_call(functools.partial(back_kernel, scale=math.pi / angles), na...  7.29 us
    ppermute x14, waiting for transfers between devices, swap(): return lax.ppermute(array, 'frame', pairs)  7.09 us
  transfers between devices with their start and end apart: 38, of which 13 were waited for; matrix products, arithmetic and copies ran while one was open for 2% of the time, Pallas kernels for 12%

profile of v3, /device:TPU:1, one launch (start us, length us, event | category | flops | bytes accessed | tf_op | source)
XLA Modules:
  0.0 276.9 jit_solution(658690415104893869)
XLA Ops:
  0.0 8.5 %shard_map.64 = (f32[24,48,128]{2,1,0:T(8,128)S(1)}, f32[24,48,128]{2,1,0:T(8,128)S(1)}, f32[24,48,128]{2,1,0:T(8,128)S(1)}, f32[24,48,128]{2,1,0:T(8,128)S(1)},...) custom-call(s32[1,96]{1,0:T(1,128)} %slot_any.3, ...), custom_call_target="tpu_custom_call" | custom-call | flops 1207959552 | bytes 19660800 | tf_op jit(solution)/shard_map/pallas_call | solution.py:152
  10.6 11.2 %shard_map.68 = (f32[24,80,128]{2,1,0:T(8,128)S(1)}, f32[24,80,128]{2,1,0:T(8,128)S(1)}, f32[24,80,128]{2,1,0:T(8,128)S(1)}, f32[24,80,128]{2,1,0:T(8,128)S(1)},...) custom-call(s32[1,96]{1,0:T(1,128)} %slot_any.3, ...), custom_call_target="tpu_custom_call" | custom-call | flops 2013265920 | bytes 24379392 | tf_op jit(solution)/shard_map/pallas_call | solution.py:152
  28.3 52.3 %collective-permute-done.1.rest_2_ = f32[24,48,128]{2,1,0:T(8,128)S(1)} collective-permute-done((f32[24,48,128]{2,1,0:T(8,128)S(1)}, f32[24,48,128]{2,1,0:T(8,128)S(1)}, u32[]{:S(2)}, u32[]{:S(2)}) %collective-permute-start.1) | collective-permute-done | bytes 589856 | tf_op jit(solution)/shard_map/ppermute | solution.py:449
  82.2 10.4 %collective-permute-done.2.rest_3_ = f32[24,48,128]{2,1,0:T(8,128)S(1)} collective-permute-done((f32[24,48,128]{2,1,0:T(8,128)S(1)}, f32[24,48,128]{2,1,0:T(8,128)S(1)}, u32[]{:S(2)}, u32[]{:S(2)}) %collective-permute-start.2) | collective-permute-done | bytes 589856 | tf_op jit(solution)/shard_map/ppermute | solution.py:449
  94.3 3.3 %collective-permute-start.7 = (f32[24,48,128]{2,1,0:T(8,128)S(1)}, f32[24,48,128]{2,1,0:T(8,128)S(1)}, u32[]{:S(2)}, u32[]{:S(2)}) collective-permute-start(f32[24,48,128]{2,1,0:T(8,128)S(1)} %get-tuple-element.63), channel_id=1, source_target_pairs={{0,8},{1,9},{2,10},{3,11},{4,12},{5,13},{6,14},{7,15},{8,0},{9,1},... | collective-permute-start | bytes 1769480 | tf_op jit(solution)/shard_map/ppermute | solution.py:449
  99.4 2.2 shard_map.69
  101.7 16.1 %collective-permute-done.6.rest_1_ = f32[24,48,128]{2,1,0:T(8,128)S(1)} collective-permute-done((f32[24,48,128]{2,1,0:T(8,128)S(1)}, f32[24,48,128]{2,1,0:T(8,128)S(1)}, u32[]{:S(2)}, u32[]{:S(2)}) %collective-permute-start.6) | collective-permute-done | bytes 589856 | tf_op jit(solution)/shard_map/ppermute | solution.py:449
  117.8 13.6 %collective-permute-done.7.rest_2_ = f32[24,48,128]{2,1,0:T(8,128)S(1)} collective-permute-done((f32[24,48,128]{2,1,0:T(8,128)S(1)}, f32[24,48,128]{2,1,0:T(8,128)S(1)}, u32[]{:S(2)}, u32[]{:S(2)}) %collective-permute-start.7) | collective-permute-done | bytes 589856 | tf_op jit(solution)/shard_map/ppermute | solution.py:449
  134.9 17.6 %collective-permute-done.26.rest_2_ = f32[24,80,128]{2,1,0:T(8,128)S(1)} collective-permute-done((f32[24,80,128]{2,1,0:T(8,128)}, f32[24,80,128]{2,1,0:T(8,128)S(1)}, u32[]{:S(2)}, u32[]{:S(2)}) %collective-permute-start.26) | collective-permute-done | bytes 983072 | tf_op jit(solution)/shard_map/ppermute | solution.py:449
  152.5 2.9 %collective-permute-start.24 = (f32[16,80,128]{2,1,0:T(8,128)S(1)}, f32[16,80,128]{2,1,0:T(8,128)S(1)}, u32[]{:S(2)}, u32[]{:S(2)}) collective-permute-start(f32[16,80,128]{2,1,0:T(8,128)S(1)} %get-tuple-element.84), channel_id=1, source_target_pairs={{0,12},{1,13},{2,14},{3,15},{4,0},{5,1},{6,2},{7,3},{8,4},{9,5},{1... | collective-permute-start | bytes 1966088 | tf_op jit(solution)/shard_map/ppermute | solution.py:449
  155.3 2.2 shard_map.70
  157.6 8.4 %collective-permute-done.8.rest_3_ = f32[24,48,128]{2,1,0:T(8,128)S(1)} collective-permute-done((f32[24,48,128]{2,1,0:T(8,128)S(1)}, f32[24,48,128]{2,1,0:T(8,128)S(1)}, u32[]{:S(2)}, u32[]{:S(2)}) %collective-permute-start.8) | collective-permute-done | bytes 589856 | tf_op jit(solution)/shard_map/ppermute | solution.py:449
  166.4 10.2 %collective-permute-done.3.refs_1_ = f32[16,48,128]{2,1,0:T(8,128)S(1)} collective-permute-done((f32[16,48,128]{2,1,0:T(8,128)S(1)}, f32[16,48,128]{2,1,0:T(8,128)S(1)}, u32[]{:S(2)}, u32[]{:S(2)}) %collective-permute-start.3) | collective-permute-done | bytes 393248 | tf_op jit(solution)/shard_map/ppermute | solution.py:449
  177.3 11.7 %collective-permute-done.23.refs_2_ = f32[16,80,128]{2,1,0:T(8,128)S(1)} collective-permute-done((f32[16,80,128]{2,1,0:T(8,128)S(1)}, f32[16,80,128]{2,1,0:T(8,128)S(1)}, u32[]{:S(2)}, u32[]{:S(2)}) %collective-permute-start.23) | collective-permute-done | bytes 655392 | tf_op jit(solution)/shard_map/ppermute | solution.py:449
  189.0 5.0 %collective-permute-done.24.refs_3_ = f32[16,80,128]{2,1,0:T(8,128)S(1)} collective-permute-done((f32[16,80,128]{2,1,0:T(8,128)S(1)}, f32[16,80,128]{2,1,0:T(8,128)S(1)}, u32[]{:S(2)}, u32[]{:S(2)}) %collective-permute-start.24) | collective-permute-done | bytes 655392 | tf_op jit(solution)/shard_map/ppermute | solution.py:449
  194.0 3.9 %collective-permute-start.5 = (f32[16,48,128]{2,1,0:T(8,128)S(1)}, f32[16,48,128]{2,1,0:T(8,128)S(1)}, u32[]{:S(2)}, u32[]{:S(2)}) collective-permute-start(f32[16,48,128]{2,1,0:T(8,128)S(1)} %get-tuple-element.60), channel_id=1, source_target_pairs={{0,12},{1,13},{2,14},{3,15},{4,0},{5,1},{6,2},{7,3},{8,4},{9,5},{1... | collective-permute-start | bytes 1179656 | tf_op jit(solution)/shard_map/ppermute | solution.py:449
  200.4 3.2 %collective-permute-start.10 = (f32[16,48,128]{2,1,0:T(8,128)S(1)}, f32[16,48,128]{2,1,0:T(8,128)S(1)}, u32[]{:S(2)}, u32[]{:S(2)}) collective-permute-start(f32[16,48,128]{2,1,0:T(8,128)S(1)} %get-tuple-element.67), channel_id=1, source_target_pairs={{0,2},{1,3},{2,0},{3,1},{4,6},{5,7},{6,4},{7,5},{8,10},{9,11},{10,... | collective-permute-start | bytes 1179656 | tf_op jit(solution)/shard_map/ppermute | solution.py:449
  205.6 3.3 %collective-permute-start.31 = (f32[4,80,128]{2,1,0:T(8,128)S(1)}, f32[4,80,128]{2,1,0:T(8,128)S(1)}, u32[]{:S(2)}, u32[]{:S(2)}) collective-permute-start(f32[4,80,128]{2,1,0:T(8,128)S(1)} %get-tuple-element.94), channel_id=1, source_target_pairs={{0,16},{16,0},{32,48},{48,32},{64,80},{80,64},{96,112},{112,96},{1... | collective-permute-start | bytes 491528 | tf_op jit(solution)/shard_map/ppermute | solution.py:457
  210.2 8.2 %collective-permute-done.10.refs_6_ = f32[16,48,128]{2,1,0:T(8,128)S(1)} collective-permute-done((f32[16,48,128]{2,1,0:T(8,128)S(1)}, f32[16,48,128]{2,1,0:T(8,128)S(1)}, u32[]{:S(2)}, u32[]{:S(2)}) %collective-permute-start.10) | collective-permute-done | bytes 393248 | tf_op jit(solution)/shard_map/ppermute | solution.py:449
  235.5 6.7 %collective-permute-done.33.rest_3_ = f32[4,80,128]{2,1,0:T(8,128)S(1)} collective-permute-done((f32[4,80,128]{2,1,0:T(8,128)S(1)}, f32[4,80,128]{2,1,0:T(8,128)S(1)}, u32[]{:S(2)}, u32[]{:S(2)}) %collective-permute-start.33) | collective-permute-done | bytes 163872 | tf_op jit(solution)/shard_map/ppermute | solution.py:457
  244.2 4.3 %collective-permute-start.17 = (f32[4,48,128]{2,1,0:T(8,128)}, f32[4,48,128]{2,1,0:T(8,128)S(1)}, u32[]{:S(2)}, u32[]{:S(2)}) collective-permute-start(f32[4,48,128]{2,1,0:T(8,128)} %copy-done.4), channel_id=1, source_target_pairs={{0,96},{16,112},{32,0},{48,16},{64,32},{80,48},{96,64},{112,80},{1... | collective-permute-start | bytes 294920 | tf_op jit(solution)/shard_map/ppermute | solution.py:457
  250.8 9.9 %tables.1 = bf16[8,4,4,256,256]{4,3,2,1,0:T(8,128)(2,1)} custom-call(s32[8,16]{1,0:T(8,128)S(1)} %copy.16.start_ref, f32[8,16,256]{2,1,0:T(8,128)S(1)} %add_add_fusion.spot_ref), custom_call_target="tpu_custom_call" | custom-call | flops 41943040 | bytes 16777216 | tf_op jit(solution)/shard_map/tables/pallas_call | solution.py:359
  263.6 5.8 %copy-done = bf16[8,4,4,256,256]{4,3,2,1,0:T(8,128)(2,1)S(1)} copy-done((bf16[8,4,4,256,256]{4,3,2,1,0:T(8,128)(2,1)S(1)}, bf16[8,4,4,256,256]{4,3,2,1,0:T(8,128)(2,1)}, u32[]{:S(2)}) %copy-start) | copy-done | bytes 16777240
  269.4 7.3 %back.1 = bf16[256,8192]{1,0:T(8,128)(2,1)} custom-call(s32[8,16]{1,0:T(8,128)S(1)} %copy.16.start_ref, bf16[4,256,512]{2,1,0:T(8,128)(2,1)S(1)} %shard_map.73.filt_ref, bf16[8,4,4,256,256]{4,3,2,1,0:T(8,128)(2,1)S(1)} %copy-done), custom_call_target="tpu_custom_call" | custom-call | flops 4294967296 | bytes 20971520 | tf_op jit(solution)/shard_map/back/pallas_call | solution.py:420
  (97 shorter events, 48.4 us)
Async XLA Ops:
  8.5 18.4 %collective-permute-start = (f32[24,48,128]{2,1,0:T(8,128)S(1)}, f32[24,48,128]{2,1,0:T(8,128)S(1)}, u32[]{:S(2)}, u32[]{:S(2)}) collective-permute-start(f32[24,48,128]{2,1,0:T(8,128)S(1)} %get-tuple-element.54), channel_id=1, source_target_pairs={{0,1},{1,2},{2,3},{3,0},{4,5},{5,6},{6,7},{7,4},{8,9},{9,10},{10,1... | collective-permute-start | bytes 1769480 | tf_op jit(solution)/shard_map/ppermute | solution.py:449
  21.8 72.5 %collective-permute-start.19 = (f32[24,80,128]{2,1,0:T(8,128)S(1)}, f32[24,80,128]{2,1,0:T(8,128)S(1)}, u32[]{:S(2)}, u32[]{:S(2)}) collective-permute-start(f32[24,80,128]{2,1,0:T(8,128)S(1)} %get-tuple-element.78), channel_id=1, source_target_pairs={{0,1},{1,2},{2,3},{3,0},{4,5},{5,6},{6,7},{7,4},{8,9},{9,10},{10,1... | collective-permute-start | bytes 2949128 | tf_op jit(solution)/shard_map/ppermute | solution.py:449
  23.1 74.5 %collective-permute-start.20 = (f32[24,80,128]{2,1,0:T(8,128)S(1)}, f32[24,80,128]{2,1,0:T(8,128)S(1)}, u32[]{:S(2)}, u32[]{:S(2)}) collective-permute-start(f32[24,80,128]{2,1,0:T(8,128)S(1)} %get-tuple-element.79), channel_id=1, source_target_pairs={{0,2},{1,3},{2,0},{3,1},{4,6},{5,7},{6,4},{7,5},{8,10},{9,11},{10,... | collective-permute-start | bytes 2949128 | tf_op jit(solution)/shard_map/ppermute | solution.py:449
  24.4 73.3 %collective-permute-start.21 = (f32[24,80,128]{2,1,0:T(8,128)S(1)}, f32[24,80,128]{2,1,0:T(8,128)S(1)}, u32[]{:S(2)}, u32[]{:S(2)}) collective-permute-start(f32[24,80,128]{2,1,0:T(8,128)S(1)} %get-tuple-element.80), channel_id=1, source_target_pairs={{0,3},{1,0},{2,1},{3,2},{4,7},{5,4},{6,5},{7,6},{8,11},{9,8},{10,9... | collective-permute-start | bytes 2949128 | tf_op jit(solution)/shard_map/ppermute | solution.py:449
  26.4 54.2 %collective-permute-start.1 = (f32[24,48,128]{2,1,0:T(8,128)S(1)}, f32[24,48,128]{2,1,0:T(8,128)S(1)}, u32[]{:S(2)}, u32[]{:S(2)}) collective-permute-start(f32[24,48,128]{2,1,0:T(8,128)S(1)} %get-tuple-element.55), channel_id=1, source_target_pairs={{0,2},{1,3},{2,0},{3,1},{4,6},{5,7},{6,4},{7,5},{8,10},{9,11},{10,... | collective-permute-start | bytes 1769480 | tf_op jit(solution)/shard_map/ppermute | solution.py:449
  26.9 65.7 %collective-permute-start.2 = (f32[24,48,128]{2,1,0:T(8,128)S(1)}, f32[24,48,128]{2,1,0:T(8,128)S(1)}, u32[]{:S(2)}, u32[]{:S(2)}) collective-permute-start(f32[24,48,128]{2,1,0:T(8,128)S(1)} %get-tuple-element.56), channel_id=1, source_target_pairs={{0,3},{1,0},{2,1},{3,2},{4,7},{5,4},{6,5},{7,6},{8,11},{9,8},{10,9... | collective-permute-start | bytes 1769480 | tf_op jit(solution)/shard_map/ppermute | solution.py:449
  80.6 52.7 %collective-permute-start.25 = (f32[24,80,128]{2,1,0:T(8,128)}, f32[24,80,128]{2,1,0:T(8,128)S(1)}, u32[]{:S(2)}, u32[]{:S(2)}) collective-permute-start(f32[24,80,128]{2,1,0:T(8,128)} %get-tuple-element.86), channel_id=1, source_target_pairs={{0,4},{1,5},{2,6},{3,7},{4,8},{5,9},{6,10},{7,11},{8,12},{9,13},{1... | collective-permute-start | bytes 2949128 | tf_op jit(solution)/shard_map/ppermute | solution.py:449
  92.7 25.1 %collective-permute-start.6 = (f32[24,48,128]{2,1,0:T(8,128)S(1)}, f32[24,48,128]{2,1,0:T(8,128)S(1)}, u32[]{:S(2)}, u32[]{:S(2)}) collective-permute-start(f32[24,48,128]{2,1,0:T(8,128)S(1)} %get-tuple-element.62), channel_id=1, source_target_pairs={{0,4},{1,5},{2,6},{3,7},{4,8},{5,9},{6,10},{7,11},{8,12},{9,13},{1... | collective-permute-start | bytes 1769480 | tf_op jit(solution)/shard_map/ppermute | solution.py:449
  94.3 37.1 %collective-permute-start.7 = (f32[24,48,128]{2,1,0:T(8,128)S(1)}, f32[24,48,128]{2,1,0:T(8,128)S(1)}, u32[]{:S(2)}, u32[]{:S(2)}) collective-permute-start(f32[24,48,128]{2,1,0:T(8,128)S(1)} %get-tuple-element.63), channel_id=1, source_target_pairs={{0,8},{1,9},{2,10},{3,11},{4,12},{5,13},{6,14},{7,15},{8,0},{9,1},... | collective-permute-start | bytes 1769480 | tf_op jit(solution)/shard_map/ppermute | solution.py:449
  97.6 54.8 %collective-permute-start.26 = (f32[24,80,128]{2,1,0:T(8,128)}, f32[24,80,128]{2,1,0:T(8,128)S(1)}, u32[]{:S(2)}, u32[]{:S(2)}) collective-permute-start(f32[24,80,128]{2,1,0:T(8,128)} %get-tuple-element.87), channel_id=1, source_target_pairs={{0,8},{1,9},{2,10},{3,11},{4,12},{5,13},{6,14},{7,15},{8,0},{9,1},... | collective-permute-start | bytes 2949128 | tf_op jit(solution)/shard_map/ppermute | solution.py:449
  97.7 54.7 %collective-permute-start.27 = (f32[24,80,128]{2,1,0:T(8,128)}, f32[24,80,128]{2,1,0:T(8,128)S(1)}, u32[]{:S(2)}, u32[]{:S(2)}) collective-permute-start(f32[24,80,128]{2,1,0:T(8,128)} %get-tuple-element.88), channel_id=1, source_target_pairs={{0,12},{1,13},{2,14},{3,15},{4,0},{5,1},{6,2},{7,3},{8,4},{9,5},{1... | collective-permute-start | bytes 2949128 | tf_op jit(solution)/shard_map/ppermute | solution.py:449
  117.8 58.9 %collective-permute-start.22 = (f32[16,80,128]{2,1,0:T(8,128)S(1)}, f32[16,80,128]{2,1,0:T(8,128)S(1)}, u32[]{:S(2)}, u32[]{:S(2)}) collective-permute-start(f32[16,80,128]{2,1,0:T(8,128)S(1)} %get-tuple-element.82), channel_id=1, source_target_pairs={{0,4},{1,5},{2,6},{3,7},{4,8},{5,9},{6,10},{7,11},{8,12},{9,13},{1... | collective-permute-start | bytes 1966088 | tf_op jit(solution)/shard_map/ppermute | solution.py:449
  131.4 34.5 %collective-permute-start.8 = (f32[24,48,128]{2,1,0:T(8,128)S(1)}, f32[24,48,128]{2,1,0:T(8,128)S(1)}, u32[]{:S(2)}, u32[]{:S(2)}) collective-permute-start(f32[24,48,128]{2,1,0:T(8,128)S(1)} %get-tuple-element.64), channel_id=1, source_target_pairs={{0,12},{1,13},{2,14},{3,15},{4,0},{5,1},{6,2},{7,3},{8,4},{9,5},{1... | collective-permute-start | bytes 1769480 | tf_op jit(solution)/shard_map/ppermute | solution.py:449
  133.3 43.3 %collective-permute-start.3 = (f32[16,48,128]{2,1,0:T(8,128)S(1)}, f32[16,48,128]{2,1,0:T(8,128)S(1)}, u32[]{:S(2)}, u32[]{:S(2)}) collective-permute-start(f32[16,48,128]{2,1,0:T(8,128)S(1)} %get-tuple-element.58), channel_id=1, source_target_pairs={{0,4},{1,5},{2,6},{3,7},{4,8},{5,9},{6,10},{7,11},{8,12},{9,13},{1... | collective-permute-start | bytes 1179656 | tf_op jit(solution)/shard_map/ppermute | solution.py:449
  152.5 36.5 %collective-permute-start.23 = (f32[16,80,128]{2,1,0:T(8,128)S(1)}, f32[16,80,128]{2,1,0:T(8,128)S(1)}, u32[]{:S(2)}, u32[]{:S(2)}) collective-permute-start(f32[16,80,128]{2,1,0:T(8,128)S(1)} %get-tuple-element.83), channel_id=1, source_target_pairs={{0,8},{1,9},{2,10},{3,11},{4,12},{5,13},{6,14},{7,15},{8,0},{9,1},... | collective-permute-start | bytes 1966088 | tf_op jit(solution)/shard_map/ppermute | solution.py:449
  152.5 41.5 %collective-permute-start.24 = (f32[16,80,128]{2,1,0:T(8,128)S(1)}, f32[16,80,128]{2,1,0:T(8,128)S(1)}, u32[]{:S(2)}, u32[]{:S(2)}) collective-permute-start(f32[16,80,128]{2,1,0:T(8,128)S(1)} %get-tuple-element.84), channel_id=1, source_target_pairs={{0,12},{1,13},{2,14},{3,15},{4,0},{5,1},{6,2},{7,3},{8,4},{9,5},{1... | collective-permute-start | bytes 1966088 | tf_op jit(solution)/shard_map/ppermute | solution.py:449
  165.9 33.9 %collective-permute-start.28 = (f32[16,80,128]{2,1,0:T(8,128)S(1)}, f32[16,80,128]{2,1,0:T(8,128)S(1)}, u32[]{:S(2)}, u32[]{:S(2)}) collective-permute-start(f32[16,80,128]{2,1,0:T(8,128)S(1)} %get-tuple-element.90), channel_id=1, source_target_pairs={{0,1},{1,2},{2,3},{3,0},{4,5},{5,6},{6,7},{7,4},{8,9},{9,10},{10,1... | collective-permute-start | bytes 1966088 | tf_op jit(solution)/shard_map/ppermute | solution.py:449
  176.7 23.7 %collective-permute-start.29 = (f32[16,80,128]{2,1,0:T(8,128)S(1)}, f32[16,80,128]{2,1,0:T(8,128)S(1)}, u32[]{:S(2)}, u32[]{:S(2)}) collective-permute-start(f32[16,80,128]{2,1,0:T(8,128)S(1)} %get-tuple-element.91), channel_id=1, source_target_pairs={{0,2},{1,3},{2,0},{3,1},{4,6},{5,7},{6,4},{7,5},{8,10},{9,11},{10,... | collective-permute-start | bytes 1966088 | tf_op jit(solution)/shard_map/ppermute | solution.py:449
  176.7 26.9 %collective-permute-start.30 = (f32[16,80,128]{2,1,0:T(8,128)S(1)}, f32[16,80,128]{2,1,0:T(8,128)S(1)}, u32[]{:S(2)}, u32[]{:S(2)}) collective-permute-start(f32[16,80,128]{2,1,0:T(8,128)S(1)} %get-tuple-element.92), channel_id=1, source_target_pairs={{0,3},{1,0},{2,1},{3,2},{4,7},{5,4},{6,5},{7,6},{8,11},{9,8},{10,9... | collective-permute-start | bytes 1966088 | tf_op jit(solution)/shard_map/ppermute | solution.py:449
  205.6 27.2 %collective-permute-start.31 = (f32[4,80,128]{2,1,0:T(8,128)S(1)}, f32[4,80,128]{2,1,0:T(8,128)S(1)}, u32[]{:S(2)}, u32[]{:S(2)}) collective-permute-start(f32[4,80,128]{2,1,0:T(8,128)S(1)} %get-tuple-element.94), channel_id=1, source_target_pairs={{0,16},{16,0},{32,48},{48,32},{64,80},{80,64},{96,112},{112,96},{1... | collective-permute-start | bytes 491528 | tf_op jit(solution)/shard_map/ppermute | solution.py:457
  208.9 25.3 %collective-permute-start.32 = (f32[4,80,128]{2,1,0:T(8,128)S(1)}, f32[4,80,128]{2,1,0:T(8,128)S(1)}, u32[]{:S(2)}, u32[]{:S(2)}) collective-permute-start(f32[4,80,128]{2,1,0:T(8,128)S(1)} %get-tuple-element.95), channel_id=1, source_target_pairs={{0,32},{16,48},{32,64},{48,80},{64,96},{80,112},{96,0},{112,16},{1... | collective-permute-start | bytes 491528 | tf_op jit(solution)/shard_map/ppermute | solution.py:457
  242.2 20.3 %collective-permute-start.14 = (f32[4,48,128]{2,1,0:T(8,128)}, f32[4,48,128]{2,1,0:T(8,128)S(1)}, u32[]{:S(2)}, u32[]{:S(2)}) collective-permute-start(f32[4,48,128]{2,1,0:T(8,128)} %copy-done.7), channel_id=1, source_target_pairs={{0,48},{16,32},{32,80},{48,64},{64,112},{80,96},{96,16},{112,0},{1... | collective-permute-start | bytes 294920 | tf_op jit(solution)/shard_map/ppermute | solution.py:457
  242.2 20.3 %collective-permute-start.15 = (f32[4,48,128]{2,1,0:T(8,128)}, f32[4,48,128]{2,1,0:T(8,128)S(1)}, u32[]{:S(2)}, u32[]{:S(2)}) collective-permute-start(f32[4,48,128]{2,1,0:T(8,128)} %copy-done.6), channel_id=1, source_target_pairs={{0,64},{16,80},{32,96},{48,112},{64,0},{80,16},{96,32},{112,48},{1... | collective-permute-start | bytes 294920 | tf_op jit(solution)/shard_map/ppermute | solution.py:457
  242.5 20.0 %collective-permute-start.16 = (f32[4,48,128]{2,1,0:T(8,128)}, f32[4,48,128]{2,1,0:T(8,128)S(1)}, u32[]{:S(2)}, u32[]{:S(2)}) collective-permute-start(f32[4,48,128]{2,1,0:T(8,128)} %copy-done.5), channel_id=1, source_target_pairs={{0,80},{16,64},{32,112},{48,96},{64,16},{80,0},{96,48},{112,32},{1... | collective-permute-start | bytes 294920 | tf_op jit(solution)/shard_map/ppermute | solution.py:457
  (23 other events, 622.0 us)
